TPU v7x, 32 devices: a whole 2x2x4 slice. The times are simulated.
32 devices in a mesh: gx: 8 (over z, x), pa: 4 (over y, core).
Axes of the slice: x: 2, y: 2, z: 4, core: 2. Of those that a mesh axis runs over, the one named last changes fastest.
Arguments:
- packed: float32 [2, 4096, 2048], P(None, 'gx', 'pa'), parts along dimension 2, may hold values from -6 to 6
- wave_y: int32 [2048], P('pa'), parts along dimension 0, may hold values from -2048 to 2047
- wave_z: int32 [2048], P('pa'), parts along dimension 0, may hold values from 1 to 2048
Outputs:
- spectra: float32 [2, 2, 4096, 2048], P(None, None, 'gx', 'pa'), parts along dimension 3
There are 4 independent parts, one for each index of `pa`. A program takes and returns all parts, laid end to end along the dimension named above; each array names one. Nothing has to cross between parts.
All inputs are finite; a program needn't handle non-finite values.
Results may differ from a plain program's by a relative error of at most 0.00007.
Values sent between devices are 32-bit elements; how exact they have to be, the bound alone decides.
No kernel may reach another device: no remote copies, remote signals or barrier semaphores. Data moves between devices by JAX's collectives and lax.ppermute only.
A program may use at most 64 MiB of HBM per device.

v0:
```python
import functools
import math

import jax
import jax.numpy as jnp
import ml_dtypes
import numpy as np
from jax import lax
from jax.experimental import pallas as pl
from jax.experimental.pallas import tpu as pltpu
from jax.sharding import PartitionSpec as P

NX = 4096
RADIX = 16
SUB = NX // RADIX
HALF_RADIX = RADIX // 2
HALF_LANES = 64
LANES = 2 * HALF_LANES
MIB = 1 << 20


def dft_tables():
    rows = np.arange(SUB)
    angles = 2.0 * np.pi * (rows[:, None] * rows[None, :] % SUB) / SUB
    matrix = np.concatenate([np.cos(angles), -np.sin(angles)]) / math.sqrt(NX)
    high = matrix.astype(np.float32).astype(ml_dtypes.bfloat16)
    low = (matrix - high.astype(np.float64)).astype(np.float32).astype(ml_dtypes.bfloat16)
    turn = 2.0 * np.pi * rows[:, None] * np.arange(RADIX)[None, :] / NX
    twiddle = np.concatenate([np.cos(turn), -np.sin(turn)], axis=1).astype(np.float32)
    return high, low, twiddle


def low_lanes(shape):
    return lax.broadcasted_iota(jnp.int32, shape, len(shape) - 1) < HALF_LANES


def swap_halves(value):
    return pltpu.roll(value, HALF_LANES, value.ndim - 1)


def pack_kernel(in_ref, out_ref):
    first, second = in_ref[0], in_ref[1]
    low = low_lanes(first.shape)
    even = jnp.where(low, first, swap_halves(second))
    odd = jnp.where(low, swap_halves(first), second)
    for side in range(2):
        out_ref[side, 0, 0] = even
        out_ref[side, 0, 1] = odd


def pack_lines(packed, chunk, side_size):
    block_len = packed.shape[1]
    tiles = side_size // 2
    rows = min(256, block_len)
    out = pl.pallas_call(
        pack_kernel,
        grid=(tiles, block_len // rows),
        in_specs=[pl.BlockSpec((2, rows, LANES), lambda t, r: (0, r, chunk * tiles + t))],
        out_specs=pl.BlockSpec((2, 1, 2, rows, LANES), lambda t, r: (0, t, 0, r, 0)),
        out_shape=jax.ShapeDtypeStruct((2, tiles, 2, block_len, LANES), jnp.float32),
        cost_estimate=pl.CostEstimate(
            flops=0, transcendentals=0, bytes_accessed=6 * side_size * block_len * LANES * 2
        ),
        name="pack_lines",
    )(packed)
    return out.reshape(2 * side_size, block_len, LANES)


def add(left, right):
    return left[0] + right[0], left[1] + right[1]


def sub(left, right):
    return left[0] - right[0], left[1] - right[1]


def turn_back(value):
    return value[1], -value[0]


def dft4(values):
    even_sum, even_dif = add(values[0], values[2]), sub(values[0], values[2])
    odd_sum, odd_dif = add(values[1], values[3]), turn_back(sub(values[1], values[3]))
    return [add(even_sum, odd_sum), add(even_dif, odd_dif), sub(even_sum, odd_sum), sub(even_dif, odd_dif)]


def dft8(values):
    root = math.sqrt(0.5)
    even, odd = dft4(values[0::2]), dft4(values[1::2])
    one = odd[1]
    three = odd[3]
    odd[1] = ((one[0] + one[1]) * root, (one[1] - one[0]) * root)
    odd[2] = turn_back(odd[2])
    odd[3] = ((three[1] - three[0]) * root, (three[0] + three[1]) * -root)
    return [add(e, o) for e, o in zip(even, odd)] + [sub(e, o) for e, o in zip(even, odd)]


def transform_kernel(meta_ref, wave_ref, high_ref, low_ref, twiddle_ref, line_ref, *rest, side_size):
    outs = rest[:side_size]
    split_high, split_low, product, result, sems = rest[side_size:]
    per_owner = HALF_RADIX // side_size
    for pair in range(RADIX // 2):
        columns = slice(2 * pair * LANES, 2 * (pair + 1) * LANES)
        for step in range(2):
            value = line_ref[pl.ds(2 * pair + step, SUB, stride=RADIX), :]
            high = value.astype(jnp.bfloat16)
            own = slice((2 * pair + step) * LANES, (2 * pair + step + 1) * LANES)
            split_high[:, own] = high
            split_low[:, own] = (value - high.astype(jnp.float32)).astype(jnp.bfloat16)
        dot = functools.partial(jnp.dot, preferred_element_type=jnp.float32)
        product[:, columns] = (
            dot(high_ref[...], split_high[:, columns])
            + dot(high_ref[...], split_low[:, columns])
            + dot(low_ref[...], split_high[:, columns])
        )

    own_place, side = meta_ref[0], meta_ref[1]
    side_float = side.astype(jnp.float32)
    sign = 1.0 - 2.0 * side_float
    along_y = jnp.broadcast_to(wave_ref[0:1, :], (8, LANES))
    cross = jnp.broadcast_to(wave_ref[1:2, :], (8, LANES))
    low = low_lanes((8, LANES))
    row_ids = lax.broadcasted_iota(jnp.int32, (8, LANES), 0).astype(jnp.float32) - 2048.0 * side_float

    def rows_body(step, carry):
        start = pl.multiple_of(step * 8, 8)
        twiddle = twiddle_ref[pl.ds(start, 8), :]
        turned = []
        for digit in range(RADIX):
            own = slice(digit * LANES, (digit + 1) * LANES)
            real = product[pl.ds(start, 8), own]
            imag = product[pl.ds(SUB + start, 8), own]
            if digit:
                cos = jnp.broadcast_to(twiddle[:, digit : digit + 1], (8, LANES))
                sin = jnp.broadcast_to(twiddle[:, RADIX + digit : RADIX + digit + 1], (8, LANES))
                real, imag = real * cos - imag * sin, real * sin + imag * cos
            turned.append((real, imag))
        even, odd = dft8(turned[0::2]), dft8(turned[1::2])
        first_row = row_ids + (step * 8).astype(jnp.float32)
        for high_digit in range(HALF_RADIX):
            angle = 2.0 * math.pi * high_digit / RADIX
            cos, sin = sign * math.cos(angle), sign * -math.sin(angle)
            e, o = even[high_digit], odd[high_digit]
            real = e[0] + (o[0] * cos - o[1] * sin)
            imag = e[1] + (o[0] * sin + o[1] * cos)
            along_x = first_row + float(high_digit * SUB)
            inverse = 1.0 / (along_x * along_x + cross)
            along = jnp.where(low, along_x, along_y)
            scaled = along * inverse
            dot_real, dot_imag = along * real, along * imag
            dot_real = dot_real + swap_halves(dot_real)
            dot_imag = dot_imag + swap_halves(dot_imag)
            result[high_digit, 0, pl.ds(start, 8), :] = real - scaled * dot_real
            result[high_digit, 1, pl.ds(start, 8), :] = imag - scaled * dot_imag
        return carry

    lax.fori_loop(0, SUB // 8, rows_body, 0)
    copies = []
    for step in range(side_size):
        owner = lax.bitwise_xor(own_place, step)
        copies.append(
            pltpu.make_async_copy(
                result.at[pl.ds(owner * per_owner, per_owner)], outs[step], sems.at[step]
            )
        )
    for copy in copies:
        copy.start()
    for copy in copies:
        copy.wait()


def transform(meta, waves, tables, lines, side_size):
    per_owner = HALF_RADIX // side_size
    vmem = pl.BlockSpec(memory_space=pltpu.VMEM)
    block = jax.ShapeDtypeStruct((per_owner, 2, SUB, LANES), jnp.float32)
    return pl.pallas_call(
        functools.partial(transform_kernel, side_size=side_size),
        in_specs=[pl.BlockSpec(memory_space=pltpu.SMEM)] + [vmem] * 5,
        out_specs=[pl.BlockSpec(memory_space=pl.ANY)] * side_size,
        out_shape=[block] * side_size,
        scratch_shapes=[
            pltpu.VMEM((SUB, RADIX * LANES), jnp.bfloat16),
            pltpu.VMEM((SUB, RADIX * LANES), jnp.bfloat16),
            pltpu.VMEM((2 * SUB, RADIX * LANES), jnp.float32),
            pltpu.VMEM((HALF_RADIX, 2, SUB, LANES), jnp.float32),
            pltpu.SemaphoreType.DMA((side_size,)),
        ],
        compiler_params=pltpu.CompilerParams(vmem_limit_bytes=32 * MIB),
        cost_estimate=pl.CostEstimate(
            flops=6 * 2 * SUB * SUB * RADIX * LANES, transcendentals=0, bytes_accessed=5 * MIB
        ),
        name="transform",
    )(meta, waves, *tables, lines)


def place_kernel(meta_ref, *refs, side_size):
    ins, out_ref = refs[:side_size], refs[-1]
    own_place = meta_ref[0]
    for part in range(2):
        held = [ref[0, part] for ref in ins]
        low = low_lanes(held[0].shape)
        blocks = []
        for source in range(side_size):
            step = lax.bitwise_xor(own_place, source)
            value = held[0]
            for other in range(1, side_size):
                value = jnp.where(step == other, held[other], value)
            blocks.append(value)
        for tile in range(side_size // 2):
            even, odd = blocks[2 * tile], blocks[2 * tile + 1]
            own = slice(tile * LANES, (tile + 1) * LANES)
            out_ref[0, part, :, own] = jnp.where(low, even, swap_halves(odd))
            out_ref[1, part, :, own] = jnp.where(low, swap_halves(even), odd)


def place(meta, blocks, before, chunk, pencils):
    side_size = len(blocks)
    per_owner = blocks[0].shape[0]
    rows = 64
    steps = SUB // rows
    width = side_size * HALF_LANES
    in_specs = [pl.BlockSpec(memory_space=pltpu.SMEM)]
    in_specs += [pl.BlockSpec((1, 2, rows, LANES), lambda q, r: (q, 0, r, 0))] * side_size
    operands = [meta, *blocks]
    aliases = {}
    if before is not None:
        in_specs.append(pl.BlockSpec(memory_space=pl.ANY))
        aliases = {len(operands): 0}
        operands.append(before)
    return pl.pallas_call(
        functools.partial(place_kernel, side_size=side_size),
        grid=(per_owner, steps),
        in_specs=in_specs,
        out_specs=pl.BlockSpec((2, 2, rows, width), lambda q, r: (0, 0, q * steps + r, chunk)),
        out_shape=jax.ShapeDtypeStruct((2, 2, per_owner * SUB, pencils), jnp.float32),
        input_output_aliases=aliases,
        cost_estimate=pl.CostEstimate(
            flops=0, transcendentals=0, bytes_accessed=8 * per_owner * 2 * SUB * LANES * side_size
        ),
        name="place",
    )(*operands)


def shards(packed, wave_y, wave_z):
    cycle_size = lax.axis_size("gx")
    side_size = cycle_size // 2
    pencils = packed.shape[2]
    chunks = pencils // (side_size * HALF_LANES)
    device_pos = lax.axis_index("gx")
    own_place = lax.rem(device_pos, side_size)
    side = device_pos // side_size
    meta = jnp.stack([own_place, side]).astype(jnp.int32)
    tables = [jnp.asarray(table) for table in dft_tables()]
    along_y = wave_y.astype(jnp.float32)
    along_z = wave_z.astype(jnp.float32)
    cross = along_y * along_y + along_z * along_z
    sends = [pack_lines(packed, chunk, side_size) for chunk in range(chunks)]
    lines = [
        lax.all_to_all(send, "gx", split_axis=0, concat_axis=0, tiled=True).reshape(NX, LANES)
        for send in sends
    ]
    result = None
    for chunk in range(chunks):
        start = (chunk * side_size + own_place) * HALF_LANES
        own_y = lax.dynamic_slice_in_dim(along_y, start, HALF_LANES)
        own_cross = lax.dynamic_slice_in_dim(cross, start, HALF_LANES)
        waves = jnp.stack([jnp.tile(own_y, 2), jnp.tile(own_cross, 2)])
        blocks = transform(meta, waves, tables, lines[chunk], side_size)
        blocks = [
            block
            if step == 0
            else lax.ppermute(block, "gx", [(i, i ^ step) for i in range(cycle_size)])
            for step, block in enumerate(blocks)
        ]
        result = place(meta, blocks, result, chunk, pencils)
    return result


def solution(mesh):
    return jax.shard_map(
        shards,
        mesh=mesh,
        in_specs=(P(None, "gx", "pa"), P("pa"), P("pa")),
        out_specs=P(None, None, "gx", "pa"),
        check_vma=False,
    )
```

profile of v0, /device:TPU:0, one launch (start us, length us, event | category | flops | bytes accessed | tf_op | source)
XLA Modules:
  0.0 157.7 jit_solution(8392992383938612466)
XLA Ops:
  0.0 3.8 %pack_lines.3 = f32[2,2,2,512,128]{4,3,2,1,0:T(8,128)} custom-call(f32[2,512,512]{2,1,0:T(8,128)} %in_ref.3), custom_call_target="tpu_custom_call" | custom-call | bytes 3145728 | tf_op jit(solution)/shard_map/pack_lines/pallas_call | solution.py:55
  3.8 7.3 %all-to-all-start.1 = ((f32[8,512,128]{2,1,0:T(8,128)}), f32[8,512,128]{2,1,0:T(8,128)S(1)}, u32[]{:S(2)}, u32[]{:S(2)}) async-start(f32[8,512,128]{2,1,0:T(8,128)} %bitcast.9), calls=%async_computation.1 | async-start | bytes 4194304 | tf_op jit(solution)/shard_map/all_to_all | solution.py:259
  11.1 3.8 %pack_lines.2 = f32[2,2,2,512,128]{4,3,2,1,0:T(8,128)} custom-call(f32[2,512,512]{2,1,0:T(8,128)} %in_ref.3), custom_call_target="tpu_custom_call" | custom-call | bytes 3145728 | tf_op jit(solution)/shard_map/pack_lines/pallas_call | solution.py:55
  14.9 44.4 %all-to-all-done.1 = f32[8,512,128]{2,1,0:T(8,128)S(1)} async-done(((f32[8,512,128]{2,1,0:T(8,128)}), f32[8,512,128]{2,1,0:T(8,128)S(1)}, u32[]{:S(2)}, u32[]{:S(2)}) %all-to-all-start.1) | async-done | bytes 2097184 | tf_op jit(solution)/shard_map/all_to_all | solution.py:259
  59.3 1.3 copy-done
  60.7 3.8 %all-to-all-start = ((f32[8,512,128]{2,1,0:T(8,128)}), f32[8,512,128]{2,1,0:T(8,128)S(1)}, u32[]{:S(2)}, u32[]{:S(2)}) async-start(f32[8,512,128]{2,1,0:T(8,128)} %bitcast.8), calls=%async_computation | async-start | bytes 4194304 | tf_op jit(solution)/shard_map/all_to_all | solution.py:259
  64.9 1.6 %copy-done.1 = f32[8,512,128]{2,1,0:T(8,128)S(1)} copy-done((f32[8,512,128]{2,1,0:T(8,128)S(1)}, f32[8,512,128]{2,1,0:T(8,128)}, u32[]{:S(2)}) %copy-start.1) | copy-done | bytes 2097176
  66.5 0.9 copy-done.6
  67.4 10.5 %transform.3 = (f32[2,2,256,128]{3,2,1,0:T(8,128)S(1)}, f32[2,2,256,128]{3,2,1,0:T(8,128)}, f32[2,2,256,128]{3,2,1,0:T(8,128)S(1)}, f32[2,2,256,128]{3,2,1,0:T(8,128)S(1)}) custom-call(s32[2]{0:T(128)S(1)} %pad_add_fusion.meta_ref, f32[2,128]{1,0:T(2,128)S(1)} %pad_maximum_fusion.1.wave_ref, bf16[512,256]{1,0:T(8,128)(2,1)S(1)} %copy-done.6, ...), custom_call_target="tpu_custom_call" | custom-call | flops 1610612736 | bytes 5242880 | tf_op jit(solution)/shard_map/transform/pallas_call | solution.py:176
  77.9 0.8 copy-done.2
  78.7 2.0 %collective-permute-start.3 = (f32[2,2,256,128]{3,2,1,0:T(8,128)}, f32[2,2,256,128]{3,2,1,0:T(8,128)}, u32[]{:S(2)}, u32[]{:S(2)}) collective-permute-start(f32[2,2,256,128]{3,2,1,0:T(8,128)} %get-tuple-element.18), channel_id=1, source_target_pairs={{0,4},{4,0},{8,12},{12,8},{16,20},{20,16},{24,28},{28,24},{1,5},{5... | collective-permute-start | bytes 1572872 | tf_op jit(solution)/shard_map/ppermute | solution.py:272
  82.1 1.5 collective-permute-start.4
  83.7 29.3 %all-to-all-done = f32[8,512,128]{2,1,0:T(8,128)S(1)} async-done(((f32[8,512,128]{2,1,0:T(8,128)}), f32[8,512,128]{2,1,0:T(8,128)S(1)}, u32[]{:S(2)}, u32[]{:S(2)}) %all-to-all-start) | async-done | bytes 2097184 | tf_op jit(solution)/shard_map/all_to_all | solution.py:259
  113.0 0.9 copy-done.7
  113.9 10.7 %transform.2 = (f32[2,2,256,128]{3,2,1,0:T(8,128)S(1)}, f32[2,2,256,128]{3,2,1,0:T(8,128)}, f32[2,2,256,128]{3,2,1,0:T(8,128)}, f32[2,2,256,128]{3,2,1,0:T(8,128)}) custom-call(s32[2]{0:T(128)S(1)} %pad_add_fusion.meta_ref, f32[2,128]{1,0:T(2,128)S(1)} %pad_maximum_fusion.wave_ref, bf16[512,256]{1,0:T(8,128)(2,1)S(1)} %copy-done.7, ...), custom_call_target="tpu_custom_call" | custom-call | flops 1610612736 | bytes 5242880 | tf_op jit(solution)/shard_map/transform/pallas_call | solution.py:176
  124.7 0.8 copy-done.3
  125.5 1.5 collective-permute-start
  126.9 2.0 %collective-permute-start.2 = (f32[2,2,256,128]{3,2,1,0:T(8,128)}, f32[2,2,256,128]{3,2,1,0:T(8,128)S(1)}, u32[]{:S(2)}, u32[]{:S(2)}) collective-permute-start(f32[2,2,256,128]{3,2,1,0:T(8,128)} %get-tuple-element.16), channel_id=1, source_target_pairs={{0,12},{4,8},{8,4},{12,0},{16,28},{20,24},{24,20},{28,16},{1,13},{... | collective-permute-start | bytes 1572872 | tf_op jit(solution)/shard_map/ppermute | solution.py:272
  129.0 6.1 %place.2.refs_4_ = f32[2,2,512,512]{3,2,1,0:T(8,128)} custom-call(s32[2]{0:T(128)} %copy-done.4, f32[2,2,256,128]{3,2,1,0:T(8,128)} %copy-done.2, f32[2,2,256,128]{3,2,1,0:T(8,128)} %collective-permute-done.3.refs_1_, f32[2,2,256,128]{3,2,1,0:T(8,128)} %collective-permute-done.4.refs_2_, f32[2,2,256,128]{3,2,1,0:T(8,128)} %collective-permute-done.5.refs_3_), custom_call_target="tpu_custom_call" | custom-call | bytes 4194304 | tf_op jit(solution)/shard_map/place/pallas_call | solution.py:230
  135.1 4.6 %collective-permute-done.refs_1_ = f32[2,2,256,128]{3,2,1,0:T(8,128)S(1)} collective-permute-done((f32[2,2,256,128]{3,2,1,0:T(8,128)}, f32[2,2,256,128]{3,2,1,0:T(8,128)S(1)}, u32[]{:S(2)}, u32[]{:S(2)}) %collective-permute-start) | collective-permute-done | bytes 524320 | tf_op jit(solution)/shard_map/ppermute | solution.py:272
  139.6 2.4 %collective-permute-done.1.refs_2_ = f32[2,2,256,128]{3,2,1,0:T(8,128)S(1)} collective-permute-done((f32[2,2,256,128]{3,2,1,0:T(8,128)}, f32[2,2,256,128]{3,2,1,0:T(8,128)S(1)}, u32[]{:S(2)}, u32[]{:S(2)}) %collective-permute-start.1) | collective-permute-done | bytes 524320 | tf_op jit(solution)/shard_map/ppermute | solution.py:272
  142.0 8.8 %collective-permute-done.2.refs_3_ = f32[2,2,256,128]{3,2,1,0:T(8,128)S(1)} collective-permute-done((f32[2,2,256,128]{3,2,1,0:T(8,128)}, f32[2,2,256,128]{3,2,1,0:T(8,128)S(1)}, u32[]{:S(2)}, u32[]{:S(2)}) %collective-permute-start.2) | collective-permute-done | bytes 524320 | tf_op jit(solution)/shard_map/ppermute | solution.py:272
  150.8 0.8 copy-done.11
  151.6 6.1 %place.3 = f32[2,2,512,512]{3,2,1,0:T(8,128)} custom-call(s32[2]{0:T(128)} %copy-done.4, f32[2,2,256,128]{3,2,1,0:T(8,128)} %copy-done.3, f32[2,2,256,128]{3,2,1,0:T(8,128)} %copy-done.9, f32[2,2,256,128]{3,2,1,0:T(8,128)} %copy-done.10, f32[2,2,256,128]{3,2,1,0:T(8,128)} %copy-done.11, f32[2,2,512,512]{3,2,1,0:T(8,128)} %place.2.refs_4_), custom_call_target="tpu_custom_call", output_to_operand_aliasing={{}: (5, {})} | custom-call | bytes 4194304 | tf_op jit(solution)/shard_map/place/pallas_call | solution.py:230
  (40 shorter events, 1.9 us)
Async XLA Ops:
  3.8 55.5 %all-to-all-start.1 = ((f32[8,512,128]{2,1,0:T(8,128)}), f32[8,512,128]{2,1,0:T(8,128)S(1)}, u32[]{:S(2)}, u32[]{:S(2)}) async-start(f32[8,512,128]{2,1,0:T(8,128)} %bitcast.9), calls=%async_computation.1 | async-start | bytes 4194304 | tf_op jit(solution)/shard_map/all_to_all | solution.py:259
  59.3 1.3 copy-start
  60.7 3.8 %copy-start.12 = (s32[512]{0:T(512)S(1)}, s32[512]{0:T(512)}, u32[]{:S(2)}) copy-start(s32[512]{0:T(512)} %param.7) | copy-start | bytes 6148
  60.7 3.8 %copy-start.13 = (s32[512]{0:T(512)S(1)}, s32[512]{0:T(512)}, u32[]{:S(2)}) copy-start(s32[512]{0:T(512)} %param.8) | copy-start | bytes 6148
  60.7 4.2 %copy-start.5 = (bf16[512,256]{1,0:T(8,128)(2,1)S(1)}, bf16[512,256]{1,0:T(8,128)(2,1)}, u32[]{:S(2)}) copy-start(bf16[512,256]{1,0:T(8,128)(2,1)} %constant.35.clone.low_ref) | copy-start | bytes 786436
  60.7 4.2 %copy-start.8 = (f32[256,32]{1,0:T(8,128)S(1)}, f32[256,32]{1,0:T(8,128)}, u32[]{:S(2)}) copy-start(f32[256,32]{1,0:T(8,128)} %constant.36.clone.twiddle_ref) | copy-start | bytes 98308
  60.7 52.3 %all-to-all-start = ((f32[8,512,128]{2,1,0:T(8,128)}), f32[8,512,128]{2,1,0:T(8,128)S(1)}, u32[]{:S(2)}, u32[]{:S(2)}) async-start(f32[8,512,128]{2,1,0:T(8,128)} %bitcast.8), calls=%async_computation | async-start | bytes 4194304 | tf_op jit(solution)/shard_map/all_to_all | solution.py:259
  64.8 48.1 %copy-start.4 = (s32[2]{0:T(128)}, s32[2]{0:T(128)S(1)}, u32[]{:S(2)}) copy-start(s32[2]{0:T(128)S(1)} %pad_add_fusion.meta_ref) | copy-start | bytes 28
  64.9 1.6 %copy-start.1 = (f32[8,512,128]{2,1,0:T(8,128)S(1)}, f32[8,512,128]{2,1,0:T(8,128)}, u32[]{:S(2)}) copy-start(f32[8,512,128]{2,1,0:T(8,128)} %copy-done) | copy-start | bytes 6291460
  66.5 0.9 copy-start.6
  77.9 0.8 copy-start.2
  78.7 48.2 %collective-permute-start.3 = (f32[2,2,256,128]{3,2,1,0:T(8,128)}, f32[2,2,256,128]{3,2,1,0:T(8,128)}, u32[]{:S(2)}, u32[]{:S(2)}) collective-permute-start(f32[2,2,256,128]{3,2,1,0:T(8,128)} %get-tuple-element.18), channel_id=1, source_target_pairs={{0,4},{4,0},{8,12},{12,8},{16,20},{20,16},{24,28},{28,24},{1,5},{5... | collective-permute-start | bytes 1572872 | tf_op jit(solution)/shard_map/ppermute | solution.py:272
  82.1 46.8 %collective-permute-start.4 = (f32[2,2,256,128]{3,2,1,0:T(8,128)S(1)}, f32[2,2,256,128]{3,2,1,0:T(8,128)}, u32[]{:S(2)}, u32[]{:S(2)}) collective-permute-start(f32[2,2,256,128]{3,2,1,0:T(8,128)S(1)} %get-tuple-element.19), channel_id=1, source_target_pairs={{0,8},{4,12},{8,0},{12,4},{16,24},{20,28},{24,16},{28,20},{1,9},{5... | collective-permute-start | bytes 1572872 | tf_op jit(solution)/shard_map/ppermute | solution.py:272
  83.6 45.3 %collective-permute-start.5 = (f32[2,2,256,128]{3,2,1,0:T(8,128)S(1)}, f32[2,2,256,128]{3,2,1,0:T(8,128)}, u32[]{:S(2)}, u32[]{:S(2)}) collective-permute-start(f32[2,2,256,128]{3,2,1,0:T(8,128)S(1)} %get-tuple-element.20), channel_id=1, source_target_pairs={{0,12},{4,8},{8,4},{12,0},{16,28},{20,24},{24,20},{28,16},{1,13},{... | collective-permute-start | bytes 1572872 | tf_op jit(solution)/shard_map/ppermute | solution.py:272
  113.0 1.0 copy-start.7
  124.7 0.8 copy-start.3
  125.5 14.2 %collective-permute-start = (f32[2,2,256,128]{3,2,1,0:T(8,128)}, f32[2,2,256,128]{3,2,1,0:T(8,128)S(1)}, u32[]{:S(2)}, u32[]{:S(2)}) collective-permute-start(f32[2,2,256,128]{3,2,1,0:T(8,128)} %get-tuple-element.14), channel_id=1, source_target_pairs={{0,4},{4,0},{8,12},{12,8},{16,20},{20,16},{24,28},{28,24},{1,5},{5... | collective-permute-start | bytes 1572872 | tf_op jit(solution)/shard_map/ppermute | solution.py:272
  126.9 15.1 %collective-permute-start.1 = (f32[2,2,256,128]{3,2,1,0:T(8,128)}, f32[2,2,256,128]{3,2,1,0:T(8,128)S(1)}, u32[]{:S(2)}, u32[]{:S(2)}) collective-permute-start(f32[2,2,256,128]{3,2,1,0:T(8,128)} %get-tuple-element.15), channel_id=1, source_target_pairs={{0,8},{4,12},{8,0},{12,4},{16,24},{20,28},{24,16},{28,20},{1,9},{5... | collective-permute-start | bytes 1572872 | tf_op jit(solution)/shard_map/ppermute | solution.py:272
  126.9 23.8 %collective-permute-start.2 = (f32[2,2,256,128]{3,2,1,0:T(8,128)}, f32[2,2,256,128]{3,2,1,0:T(8,128)S(1)}, u32[]{:S(2)}, u32[]{:S(2)}) collective-permute-start(f32[2,2,256,128]{3,2,1,0:T(8,128)} %get-tuple-element.16), channel_id=1, source_target_pairs={{0,12},{4,8},{8,4},{12,0},{16,28},{20,24},{24,20},{28,16},{1,13},{... | collective-permute-start | bytes 1572872 | tf_op jit(solution)/shard_map/ppermute | solution.py:272
  139.6 11.1 %copy-start.9 = (f32[2,2,256,128]{3,2,1,0:T(8,128)}, f32[2,2,256,128]{3,2,1,0:T(8,128)S(1)}, u32[]{:S(2)}) copy-start(f32[2,2,256,128]{3,2,1,0:T(8,128)S(1)} %collective-permute-done.refs_1_) | copy-start | bytes 1572868
  142.0 8.8 %copy-start.10 = (f32[2,2,256,128]{3,2,1,0:T(8,128)}, f32[2,2,256,128]{3,2,1,0:T(8,128)S(1)}, u32[]{:S(2)}) copy-start(f32[2,2,256,128]{3,2,1,0:T(8,128)S(1)} %collective-permute-done.1.refs_2_) | copy-start | bytes 1572868
  150.8 0.8 copy-start.11
where the time goes:
time: 159 us; the launch traced here: 158 us
  waiting for transfers between devices  89.4 us (56%)
  Pallas kernels  41.1 us (26%)
  starting transfers between devices  18.1 us (11%)
  local copies, waits for them, and re-layouts  8.88 us (6%)
    all_to_all x2, waiting for transfers between devices, shards(): lax.all_to_all(send, 'gx', split_axis=0, concat_axis=0, tiled=True)  73.7 us
    pallas_call x2, Pallas kernels, transform(): pl.pallas_call(functools.partial(transform_kernel, side_size=side_size),...  21.2 us
    ppermute x6, waiting for transfers between devices, shards(): lax.ppermute(block, 'gx', [(i, i ^ step) for i in range(cycle_size)])  15.7 us
    pallas_call x2, Pallas kernels, place(): pl.pallas_call(functools.partial(place_kernel, side_size=side_size), grid...  12.2 us
    all_to_all x2, starting transfers between devices, shards(): lax.all_to_all(send, 'gx', split_axis=0, concat_axis=0, tiled=True)  11 us
    pallas_call x2, Pallas kernels, pack_lines(): pl.pallas_call(pack_kernel, grid=(tiles, block_len // rows), in_specs=[pl...  7.66 us
    unnamed x28, local copies, waits for them, and re-layouts  7.22 us
    ppermute x6, starting transfers between devices, shards(): lax.ppermute(block, 'gx', [(i, i ^ step) for i in range(cycle_size)])  7.09 us
  transfers between devices with their start and end apart: 8, of which 5 were waited for; matrix products, arithmetic and copies ran while one was open for 1% of the time, Pallas kernels for 20%

commit v1 on v0

v1 whole, which is shorter than its diff:
```python
import functools
import math

import jax
import jax.numpy as jnp
import ml_dtypes
import numpy as np
from jax import lax
from jax.experimental import pallas as pl
from jax.experimental.pallas import tpu as pltpu
from jax.sharding import PartitionSpec as P

NX = 4096
RADIX = 16
SUB = NX // RADIX
HALF_RADIX = RADIX // 2
HALF_LANES = 64
LANES = 2 * HALF_LANES
MIB = 1 << 20


def dft_tables():
    rows = np.arange(SUB)
    angles = 2.0 * np.pi * (rows[:, None] * rows[None, :] % SUB) / SUB
    matrix = np.concatenate([np.cos(angles), -np.sin(angles)]) / math.sqrt(NX)
    high = matrix.astype(np.float32).astype(ml_dtypes.bfloat16)
    low = (matrix - high.astype(np.float64)).astype(np.float32).astype(ml_dtypes.bfloat16)
    turn = 2.0 * np.pi * rows[:, None] * np.arange(RADIX)[None, :] / NX
    twiddle = np.concatenate([np.cos(turn), -np.sin(turn)], axis=1).astype(np.float32)
    return high, low, twiddle


def low_lanes(shape):
    return lax.broadcasted_iota(jnp.int32, shape, len(shape) - 1) < HALF_LANES


def swap_halves(value):
    return pltpu.roll(value, HALF_LANES, value.ndim - 1)


def pack_kernel(meta_ref, in_hbm, *rest, side_size, plan):
    outs, (lines, mixed, sems) = rest[:-3], rest[-3:]
    tiles = side_size // 2
    chunks = sorted({chunk for targets in plan for _, chunk, _, _ in targets})
    loads = {}
    for chunk in chunks:
        for tile in range(tiles):
            columns = pl.ds((chunk * tiles + tile) * LANES, LANES)
            slot = len(loads)
            loads[chunk, tile] = pltpu.make_async_copy(
                in_hbm.at[:, :, columns], lines.at[slot], sems.at[slot]
            )
            loads[chunk, tile].start()
    stores = []
    for index, chunk in enumerate(chunks):
        for tile in range(tiles):
            loads[chunk, tile].wait()
            slot = index * tiles + tile
            first, second = lines[slot, 0], lines[slot, 1]
            low = low_lanes(first.shape)
            moved = swap_halves(jnp.where(low, second, first))
            mixed[index, 2 * tile] = jnp.where(low, first, moved)
            mixed[index, 2 * tile + 1] = jnp.where(low, moved, second)
        for out, targets in zip(outs, plan):
            for spot, own_chunk, owner, relative in targets:
                if own_chunk == chunk:
                    if relative:
                        owner = lax.bitwise_xor(meta_ref[0], owner)
                    stores.append(
                        pltpu.make_async_copy(
                            mixed.at[index, owner], out.at[spot], sems.at[len(loads) + len(stores)]
                        )
                    )
                    stores[-1].start()
    for store in stores:
        store.wait()


def pack_lines(meta, packed, side_size, plan, shapes):
    block_len = packed.shape[1]
    tiles = side_size // 2
    hbm = pl.BlockSpec(memory_space=pl.ANY)
    chunks = len({chunk for targets in plan for _, chunk, _, _ in targets})
    copies = sum(len(targets) for targets in plan)
    return pl.pallas_call(
        functools.partial(pack_kernel, side_size=side_size, plan=plan),
        in_specs=[pl.BlockSpec(memory_space=pltpu.SMEM), hbm],
        out_specs=[hbm] * len(plan),
        out_shape=[
            jax.ShapeDtypeStruct((*shape, block_len, LANES), jnp.float32) for shape in shapes
        ],
        scratch_shapes=[
            pltpu.VMEM((chunks * tiles, 2, block_len, LANES), jnp.float32),
            pltpu.VMEM((chunks, side_size, block_len, LANES), jnp.float32),
            pltpu.SemaphoreType.DMA((chunks * tiles + copies,)),
        ],
        cost_estimate=pl.CostEstimate(
            flops=0,
            transcendentals=0,
            bytes_accessed=4 * block_len * LANES * (chunks * side_size + copies),
        ),
        name="pack_lines",
    )(meta, packed)


def add(left, right):
    return left[0] + right[0], left[1] + right[1]


def sub(left, right):
    return left[0] - right[0], left[1] - right[1]


def turn_back(value):
    return value[1], -value[0]


def dft4(values):
    even_sum, even_dif = add(values[0], values[2]), sub(values[0], values[2])
    odd_sum, odd_dif = add(values[1], values[3]), turn_back(sub(values[1], values[3]))
    return [add(even_sum, odd_sum), add(even_dif, odd_dif), sub(even_sum, odd_sum), sub(even_dif, odd_dif)]


def dft8(values):
    root = math.sqrt(0.5)
    even, odd = dft4(values[0::2]), dft4(values[1::2])
    one = odd[1]
    three = odd[3]
    odd[1] = ((one[0] + one[1]) * root, (one[1] - one[0]) * root)
    odd[2] = turn_back(odd[2])
    odd[3] = ((three[1] - three[0]) * root, (three[0] + three[1]) * -root)
    return [add(e, o) for e, o in zip(even, odd)] + [sub(e, o) for e, o in zip(even, odd)]


def transform_kernel(
    meta_ref, wave_y_ref, wave_z_ref, high_ref, low_ref, twiddle_hbm, *rest, chunk, side_size, spots
):
    operands = 1 + max(operand for operand, _, _, _ in spots)
    inputs, rest = rest[:operands], rest[operands:]
    outs = rest[:side_size]
    split_high, split_low, product, result, twiddle, line, sems, line_sems = rest[side_size:]
    block_len = inputs[0].shape[-2]
    span = block_len // RADIX
    device_pos = meta_ref[1] * side_size + meta_ref[0]
    per_owner = HALF_RADIX // side_size
    load = pltpu.make_async_copy(twiddle_hbm, twiddle, sems.at[side_size])
    load.start()
    fetches, targets = [], []
    for step, (operand, spot, place, relative) in enumerate(spots):
        rows = pl.ds(place * span, span)
        if relative:
            source = lax.bitwise_xor(device_pos, place)
            fetches.append(
                pltpu.make_async_copy(
                    inputs[operand].at[spot], line.at[source], line_sems.at[step]
                )
            )
            fetches[-1].start()
            targets.append((line, place, rows))
        else:
            targets.append((inputs[operand], spot, rows))
    for fetch in fetches:
        fetch.wait()
    dot = functools.partial(jnp.dot, preferred_element_type=jnp.float32)
    for pair in range(RADIX // 2):
        columns = slice(2 * pair * LANES, 2 * (pair + 1) * LANES)
        for digit in (2 * pair, 2 * pair + 1):
            own = slice(digit * LANES, (digit + 1) * LANES)
            for ref, spot, rows in targets:
                value = ref[spot, pl.ds(digit, span, stride=RADIX), :]
                high = value.astype(jnp.bfloat16)
                split_high[rows, own] = high
                split_low[rows, own] = (value - high.astype(jnp.float32)).astype(jnp.bfloat16)
        product[:, columns] = (
            dot(high_ref[...], split_high[:, columns])
            + dot(high_ref[...], split_low[:, columns])
            + dot(low_ref[...], split_high[:, columns])
        )

    own_place = meta_ref[0]
    side_float = meta_ref[1].astype(jnp.float32)
    sign = 1.0 - 2.0 * side_float
    low = low_lanes((8, LANES))
    group = chunk * side_size + own_place
    keep = (lax.broadcasted_iota(jnp.int32, (1, LANES), 1) < HALF_LANES) == (group % 2 == 0)

    def own_lanes(ref):
        tile = ref[pl.ds(group // 2, 1), :].astype(jnp.float32)
        return jnp.where(keep, tile, swap_halves(tile))

    own_y, own_z = own_lanes(wave_y_ref), own_lanes(wave_z_ref)
    along_y = jnp.broadcast_to(own_y, (8, LANES))
    cross = jnp.broadcast_to(own_y * own_y + own_z * own_z, (8, LANES))
    row_ids = lax.broadcasted_iota(jnp.int32, (8, LANES), 0).astype(jnp.float32) - 2048.0 * side_float
    load.wait()

    def rows_body(step, carry):
        start = pl.multiple_of(step * 8, 8)
        turned = []
        for digit in range(RADIX):
            own = slice(digit * LANES, (digit + 1) * LANES)
            real = product[pl.ds(start, 8), own]
            imag = product[pl.ds(SUB + start, 8), own]
            if digit:
                cos = twiddle[digit, pl.ds(start, 8), :]
                sin = twiddle[RADIX + digit, pl.ds(start, 8), :]
                real, imag = real * cos - imag * sin, real * sin + imag * cos
            turned.append((real, imag))
        even, odd = dft8(turned[0::2]), dft8(turned[1::2])
        first_row = row_ids + (step * 8).astype(jnp.float32)
        for high_digit in range(HALF_RADIX):
            angle = 2.0 * math.pi * high_digit / RADIX
            cos, sin = sign * math.cos(angle), sign * -math.sin(angle)
            e, o = even[high_digit], odd[high_digit]
            real = e[0] + (o[0] * cos - o[1] * sin)
            imag = e[1] + (o[0] * sin + o[1] * cos)
            along_x = first_row + float(high_digit * SUB)
            inverse = 1.0 / (along_x * along_x + cross)
            along = jnp.where(low, along_x, along_y)
            scaled = along * inverse
            dot_real, dot_imag = along * real, along * imag
            dot_real = dot_real + swap_halves(dot_real)
            dot_imag = dot_imag + swap_halves(dot_imag)
            result[high_digit, 0, pl.ds(start, 8), :] = real - scaled * dot_real
            result[high_digit, 1, pl.ds(start, 8), :] = imag - scaled * dot_imag
        return carry

    copies = []
    parts = 2
    for part in range(parts):
        steps = SUB // 8 // parts
        lax.fori_loop(part * steps, (part + 1) * steps, rows_body, 0, unroll=UNROLL)
        rows = pl.ds(part * SUB // parts, SUB // parts)
        for step in range(side_size):
            owner = lax.bitwise_xor(own_place, step)
            copies.append(
                pltpu.make_async_copy(
                    result.at[pl.ds(owner * per_owner, per_owner), :, rows],
                    outs[step].at[:, :, rows],
                    sems.at[step + part * (side_size + 1)],
                )
            )
            copies[-1].start()
    for copy in copies:
        copy.wait()


UNROLL = 4


def transform(meta, wave_y, wave_z, tables, arrays, spots, chunk, side_size):
    per_owner = HALF_RADIX // side_size
    vmem = pl.BlockSpec(memory_space=pltpu.VMEM)
    hbm = pl.BlockSpec(memory_space=pl.ANY)
    block = jax.ShapeDtypeStruct((per_owner, 2, SUB, LANES), jnp.float32)
    return pl.pallas_call(
        functools.partial(transform_kernel, chunk=chunk, side_size=side_size, spots=spots),
        in_specs=[pl.BlockSpec(memory_space=pltpu.SMEM)] + [vmem] * 4 + [hbm] + [vmem] * len(arrays),
        out_specs=[hbm] * side_size,
        out_shape=[block] * side_size,
        scratch_shapes=[
            pltpu.VMEM((SUB, RADIX * LANES), jnp.bfloat16),
            pltpu.VMEM((SUB, RADIX * LANES), jnp.bfloat16),
            pltpu.VMEM((2 * SUB, RADIX * LANES), jnp.float32),
            pltpu.VMEM((HALF_RADIX, 2, SUB, LANES), jnp.float32),
            pltpu.VMEM((2 * RADIX, SUB, LANES), jnp.float32),
            pltpu.VMEM((2 * side_size, NX // (2 * side_size), LANES), jnp.float32),
            pltpu.SemaphoreType.DMA((2 * side_size + 1,)),
            pltpu.SemaphoreType.DMA((2 * side_size,)),
        ],
        compiler_params=pltpu.CompilerParams(vmem_limit_bytes=24 * MIB),
        cost_estimate=pl.CostEstimate(
            flops=6 * 2 * SUB * SUB * RADIX * LANES, transcendentals=0, bytes_accessed=5 * MIB
        ),
        name="transform",
    )(meta, wave_y, wave_z, *tables, *arrays)


def place_kernel(meta_ref, even_ref, odd_ref, *rest, chunk, step, side_size):
    out_hbm, mixed, sems = rest[-3:]
    own_place = meta_ref[0]
    tile = chunk * (side_size // 2) + lax.bitwise_xor(own_place // 2, step)
    ordered = own_place % 2 == 0
    columns = pl.ds(pl.multiple_of(tile * LANES, LANES), LANES)
    rows = SUB // PARTS
    stores = []
    for part in range(mixed.shape[0] * PARTS):
        index, own = part // PARTS, pl.ds(part % PARTS * rows, rows)
        first, second = even_ref[index, :, own], odd_ref[index, :, own]
        even = jnp.where(ordered, first, second)
        odd = jnp.where(ordered, second, first)
        low = low_lanes(even.shape)
        moved = swap_halves(jnp.where(low, odd, even))
        mixed[index, 0, :, own] = jnp.where(low, even, moved)
        mixed[index, 1, :, own] = jnp.where(low, moved, odd)
        stores.append(
            pltpu.make_async_copy(
                mixed.at[index, :, :, own],
                out_hbm.at[:, :, pl.ds(part * rows, rows), columns],
                sems.at[part],
            )
        )
        stores[-1].start()
    for store in stores:
        store.wait()


PARTS = 2


def place(meta, pair, before, chunk, step, side_size, pencils):
    per_owner = pair[0].shape[0]
    vmem = pl.BlockSpec(memory_space=pltpu.VMEM)
    hbm = pl.BlockSpec(memory_space=pl.ANY)
    operands = [meta, *pair]
    aliases = {}
    if before is not None:
        aliases = {len(operands): 0}
        operands.append(before)
    return pl.pallas_call(
        functools.partial(place_kernel, chunk=chunk, step=step, side_size=side_size),
        in_specs=[pl.BlockSpec(memory_space=pltpu.SMEM)] + [vmem] * 2 + [hbm] * (len(operands) - 3),
        out_specs=hbm,
        out_shape=jax.ShapeDtypeStruct((2, 2, per_owner * SUB, pencils), jnp.float32),
        scratch_shapes=[
            pltpu.VMEM((per_owner, 2, 2, SUB, LANES), jnp.float32),
            pltpu.SemaphoreType.DMA((PARTS * per_owner,)),
        ],
        input_output_aliases=aliases,
        compiler_params=pltpu.CompilerParams(vmem_limit_bytes=8 * MIB),
        cost_estimate=pl.CostEstimate(
            flops=0, transcendentals=0, bytes_accessed=16 * per_owner * 2 * SUB * LANES
        ),
        name="place",
    )(*operands)


def shards(packed, wave_y, wave_z):
    cycle_size = lax.axis_size("gx")
    side_size = cycle_size // 2
    block_len, pencils = packed.shape[1:]
    chunks = pencils // (side_size * HALF_LANES)
    device_pos = lax.axis_index("gx")
    own_place = lax.rem(device_pos, side_size)
    side = device_pos // side_size
    meta = jnp.stack([own_place, side]).astype(jnp.int32)
    high, low, twiddle = dft_tables()
    twiddle = jnp.broadcast_to(jnp.asarray(twiddle.T)[:, :, None], (2 * RADIX, SUB, LANES))
    tables = [jnp.asarray(high), jnp.asarray(low), twiddle]
    wave_y = wave_y.reshape(pencils // LANES, LANES)
    wave_z = wave_z.reshape(pencils // LANES, LANES)

    def swap(value, step):
        return lax.ppermute(value, "gx", [(i, i ^ step) for i in range(cycle_size)])

    places = list(range(side_size))
    first_plan = [[((side, place), 0, place, False) for side in range(2) for place in places]]
    (send,) = pack_lines(meta, packed, side_size, first_plan, [(2, side_size)])
    got = lax.all_to_all(
        send.reshape(cycle_size, block_len, LANES), "gx", split_axis=0, concat_axis=0, tiled=True
    )
    lines = [([got], [(0, place, place, False) for place in range(cycle_size)])]
    for chunk in range(1, chunks):
        (send,), packed = lax.optimization_barrier(((send,), packed))
        near_plan = [[(0, chunk, place, True)] for place in places]
        near = pack_lines(meta, packed, side_size, near_plan, [(1,)] * side_size)
        near = [near[0]] + [swap(near[place], place) for place in places[1:]]
        held = jnp.concatenate(near)
        got, held = lax.optimization_barrier((got, held))
        lines[0] = ([got], lines[0][1])
        far = swap(held, side_size)
        spots = [(0, place, place, True) for place in places]
        spots += [(1, place, side_size + place, True) for place in places]
        lines.append(([held, far], spots))
    result = None
    for chunk in range(chunks):
        blocks = transform(meta, wave_y, wave_z, tables, *lines[chunk], chunk, side_size)
        blocks = [
            block
            if step == 0
            else lax.ppermute(block, "gx", [(i, i ^ step) for i in range(cycle_size)])
            for step, block in enumerate(blocks)
        ]
        for step in range(side_size // 2):
            pair = blocks[2 * step : 2 * step + 2]
            result = place(meta, pair, result, chunk, step, side_size, pencils)
    return result


def solution(mesh):
    return jax.shard_map(
        shards,
        mesh=mesh,
        in_specs=(P(None, "gx", "pa"), P("pa"), P("pa")),
        out_specs=P(None, None, "gx", "pa"),
        check_vma=False,
    )
```

time: 159 us -> 141 us (0.89)
  Pallas kernels: 41.1 us -> 24.9 us
  local copies, waits for them, and re-layouts: 8.88 us -> 1.17 us
  starting transfers between devices: 18.1 us -> 21.5 us
  waiting for transfers between devices: 89.4 us -> 91 us
    ppermute x0 -> x4, waiting for transfers between devices: none -> 73.6 us  [swap(): return lax.ppermute(value, 'gx', [(i, i ^ step) for i in range(cycle_size)])]
    all_to_all x2 -> x1, waiting for transfers between devices: 73.7 us -> 0.91 us  [shards(): lax.all_to_all(send.reshape(cycle_size, block_len, LANES), 'gx', split_ax...]
    pallas_call x6 -> x8, Pallas kernels: 41.1 us -> 24.9 us  [the longest x2 11.6 us: transform(): pl.pallas_call(functools.partial(transform_kernel, chunk=chunk, side_size...]
    unnamed x28 -> x12, local copies, waits for them, and re-layouts: 7.22 us -> 0.03 us
    ppermute x0 -> x4, starting transfers between devices: none -> 7.17 us  [swap(): return lax.ppermute(value, 'gx', [(i, i ^ step) for i in range(cycle_size)])]
    all_to_all x2 -> x1, starting transfers between devices: 11 us -> 7.26 us  [shards(): lax.all_to_all(send.reshape(cycle_size, block_len, LANES), 'gx', split_ax...]
  transfers between devices with their start and end apart: 8 -> 11, of which waited for: 5 -> 7; matrix products, arithmetic and copies ran while one was open for 1% -> 2% of each run, Pallas kernels for 20% -> 14%
where the time goes in v1:
time: 141 us; the launch traced here: 140 us
  waiting for transfers between devices  91 us (65%)
  Pallas kernels  24.9 us (18%)
  starting transfers between devices  21.5 us (15%)
  other arithmetic  1.67 us (1%)
    ppermute x4, waiting for transfers between devices, swap(): return lax.ppermute(value, 'gx', [(i, i ^ step) for i in range(cycle_size)])  73.6 us
    ppermute x6, waiting for transfers between devices, shards(): lax.ppermute(block, 'gx', [(i, i ^ step) for i in range(cycle_size)])  16.5 us
    pallas_call x2, Pallas kernels, transform(): pl.pallas_call(functools.partial(transform_kernel, chunk=chunk, side_size...  11.6 us
    all_to_all x1, starting transfers between devices, shards(): lax.all_to_all(send.reshape(cycle_size, block_len, LANES), 'gx', split_ax...  7.26 us
    ppermute x4, starting transfers between devices, swap(): return lax.ppermute(value, 'gx', [(i, i ^ step) for i in range(cycle_size)])  7.17 us
    ppermute x6, starting transfers between devices, shards(): lax.ppermute(block, 'gx', [(i, i ^ step) for i in range(cycle_size)])  7.11 us
    pallas_call x4, Pallas kernels, place(): pl.pallas_call(functools.partial(place_kernel, chunk=chunk, step=step, si...  6.81 us
    pallas_call x2, Pallas kernels, pack_lines(): pl.pallas_call(functools.partial(pack_kernel, side_size=side_size, plan=p...  6.58 us
  transfers between devices with their start and end apart: 11, of which 7 were waited for; matrix products, arithmetic and copies ran while one was open for 2% of the time, Pallas kernels for 14%

profile of v1, /device:TPU:0, one launch (start us, length us, event | category | flops | bytes accessed | tf_op | source)
XLA Modules:
  0.0 140.5 jit_solution(12901074027646717383)
XLA Ops:
  0.7 3.4 %pack_lines.2 = f32[2,4,512,128]{3,2,1,0:T(8,128)} custom-call(s32[2]{0:T(128)} %pad_add_fusion.meta_ref, f32[2,512,512]{2,1,0:T(8,128)} %in_hbm.2), custom_call_target="tpu_custom_call" | custom-call | bytes 3145728 | tf_op jit(solution)/shard_map/pack_lines/pallas_call | solution.py:85
  4.1 7.3 %all-to-all-start = ((f32[8,512,128]{2,1,0:T(8,128)}), f32[8,512,128]{2,1,0:T(8,128)S(1)}, u32[]{:S(2)}, u32[]{:S(2)}) async-start(f32[8,512,128]{2,1,0:T(8,128)} %bitcast.9), calls=%async_computation | async-start | bytes 4194304 | tf_op jit(solution)/shard_map/all_to_all | solution.py:359
  11.4 3.2 %pack_lines.3 = (f32[1,512,128]{2,1,0:T(8,128)}, f32[1,512,128]{2,1,0:T(8,128)}, f32[1,512,128]{2,1,0:T(8,128)}, f32[1,512,128]{2,1,0:T(8,128)}) custom-call(s32[2]{0:T(128)} %pad_add_fusion.meta_ref, f32[2,512,512]{2,1,0:T(8,128)} %in_hbm.2), custom_call_target="tpu_custom_call" | custom-call | bytes 2097152 | tf_op jit(solution)/shard_map/pack_lines/pallas_call | solution.py:85
  14.6 2.1 %collective-permute-start = (f32[1,512,128]{2,1,0:T(8,128)}, f32[1,512,128]{2,1,0:T(8,128)S(1)}, u32[]{:S(2)}, u32[]{:S(2)}) collective-permute-start(f32[1,512,128]{2,1,0:T(8,128)} %get-tuple-element.22), channel_id=1, source_target_pairs={{0,4},{4,0},{8,12},{12,8},{16,20},{20,16},{24,28},{28,24},{1,5},{5... | collective-permute-start | bytes 786440 | tf_op jit(solution)/shard_map/ppermute | solution.py:354
  16.6 1.5 %collective-permute-start.1 = (f32[1,512,128]{2,1,0:T(8,128)}, f32[1,512,128]{2,1,0:T(8,128)S(1)}, u32[]{:S(2)}, u32[]{:S(2)}) collective-permute-start(f32[1,512,128]{2,1,0:T(8,128)} %get-tuple-element.23), channel_id=1, source_target_pairs={{0,8},{4,12},{8,0},{12,4},{16,24},{20,28},{24,16},{28,20},{1,9},{5... | collective-permute-start | bytes 786440 | tf_op jit(solution)/shard_map/ppermute | solution.py:354
  18.2 17.1 %collective-permute-done = f32[1,512,128]{2,1,0:T(8,128)S(1)} collective-permute-done((f32[1,512,128]{2,1,0:T(8,128)}, f32[1,512,128]{2,1,0:T(8,128)S(1)}, u32[]{:S(2)}, u32[]{:S(2)}) %collective-permute-start) | collective-permute-done | bytes 262176 | tf_op jit(solution)/shard_map/ppermute | solution.py:354
  35.3 17.9 %collective-permute-done.1 = f32[1,512,128]{2,1,0:T(8,128)S(1)} collective-permute-done((f32[1,512,128]{2,1,0:T(8,128)}, f32[1,512,128]{2,1,0:T(8,128)S(1)}, u32[]{:S(2)}, u32[]{:S(2)}) %collective-permute-start.1) | collective-permute-done | bytes 262176 | tf_op jit(solution)/shard_map/ppermute | solution.py:354
  53.2 4.5 %collective-permute-done.2 = f32[1,512,128]{2,1,0:T(8,128)S(1)} collective-permute-done((f32[1,512,128]{2,1,0:T(8,128)}, f32[1,512,128]{2,1,0:T(8,128)S(1)}, u32[]{:S(2)}, u32[]{:S(2)}) %collective-permute-start.2) | collective-permute-done | bytes 262176 | tf_op jit(solution)/shard_map/ppermute | solution.py:354
  57.6 1.0 pad_maximum_fusion.rest_0_
  58.7 0.9 all-to-all-done.rest_0_
  59.6 3.6 %collective-permute-start.3 = (f32[4,512,128]{2,1,0:T(8,128)S(1)}, f32[4,512,128]{2,1,0:T(8,128)S(1)}, u32[]{:S(2)}, u32[]{:S(2)}) collective-permute-start(f32[4,512,128]{2,1,0:T(8,128)S(1)} %pad_maximum_fusion.rest_0_), channel_id=1, source_target_pairs={{0,16},{4,20},{8,24},{12,28},{16,0},{20,4},{24,8},{28,12},{1,17},{... | collective-permute-start | bytes 3145736 | tf_op jit(solution)/shard_map/ppermute | solution.py:354
  63.1 1.1 broadcast_in_dim.2.twiddle_hbm
  64.3 5.7 %transform.3 = (f32[2,2,256,128]{3,2,1,0:T(8,128)S(1)}, f32[2,2,256,128]{3,2,1,0:T(8,128)S(1)}, f32[2,2,256,128]{3,2,1,0:T(8,128)S(1)}, f32[2,2,256,128]{3,2,1,0:T(8,128)S(1)}) custom-call(s32[2]{0:T(128)S(1)} %copy-done.2, s32[4,128]{1,0:T(4,128)S(1)} %bitcast.5, s32[4,128]{1,0:T(4,128)S(1)} %bitcast.7, bf16[512,256]{1,0:T(8,128)(2,1)S(1)} %copy-done.1, ...), custom_call_target="tpu_custom_call" | custom-call | flops 1610612736 | bytes 5242880 | tf_op jit(solution)/shard_map/transform/pallas_call | solution.py:256
  70.7 2.9 %collective-permute-start.8 = (f32[2,2,256,128]{3,2,1,0:T(8,128)S(1)}, f32[2,2,256,128]{3,2,1,0:T(8,128)S(1)}, u32[]{:S(2)}, u32[]{:S(2)}) collective-permute-start(f32[2,2,256,128]{3,2,1,0:T(8,128)S(1)} %get-tuple-element.32), channel_id=1, source_target_pairs={{0,12},{4,8},{8,4},{12,0},{16,28},{20,24},{24,20},{28,16},{1,13},{... | collective-permute-start | bytes 1572872 | tf_op jit(solution)/shard_map/ppermute | solution.py:381
  73.6 34.1 %collective-permute-done.3.rest_1_ = f32[4,512,128]{2,1,0:T(8,128)S(1)} collective-permute-done((f32[4,512,128]{2,1,0:T(8,128)S(1)}, f32[4,512,128]{2,1,0:T(8,128)S(1)}, u32[]{:S(2)}, u32[]{:S(2)}) %collective-permute-start.3) | collective-permute-done | bytes 1048608 | tf_op jit(solution)/shard_map/ppermute | solution.py:354
  107.7 5.8 %transform.2 = (f32[2,2,256,128]{3,2,1,0:T(8,128)S(1)}, f32[2,2,256,128]{3,2,1,0:T(8,128)S(1)}, f32[2,2,256,128]{3,2,1,0:T(8,128)S(1)}, f32[2,2,256,128]{3,2,1,0:T(8,128)S(1)}) custom-call(s32[2]{0:T(128)S(1)} %copy-done.2, s32[4,128]{1,0:T(4,128)S(1)} %bitcast.6, s32[4,128]{1,0:T(4,128)S(1)} %bitcast.8, bf16[512,256]{1,0:T(8,128)(2,1)S(1)} %copy-done.1, ...), custom_call_target="tpu_custom_call" | custom-call | flops 1610612736 | bytes 5242880 | tf_op jit(solution)/shard_map/transform/pallas_call | solution.py:256
  113.6 1.0 collective-permute-start.6
  114.5 2.6 %collective-permute-start.5 = (f32[2,2,256,128]{3,2,1,0:T(8,128)S(1)}, f32[2,2,256,128]{3,2,1,0:T(8,128)S(1)}, u32[]{:S(2)}, u32[]{:S(2)}) collective-permute-start(f32[2,2,256,128]{3,2,1,0:T(8,128)S(1)} %get-tuple-element.27), channel_id=1, source_target_pairs={{0,12},{4,8},{8,4},{12,0},{16,28},{20,24},{24,20},{28,16},{1,13},{... | collective-permute-start | bytes 1572872 | tf_op jit(solution)/shard_map/ppermute | solution.py:381
  117.1 1.7 %place.4.rest_0_ = f32[2,2,512,512]{3,2,1,0:T(8,128)} custom-call(s32[2]{0:T(128)S(1)} %copy-done.2, f32[2,2,256,128]{3,2,1,0:T(8,128)S(1)} %get-tuple-element.33.even_ref, f32[2,2,256,128]{3,2,1,0:T(8,128)S(1)} %collective-permute-done.9.odd_ref), custom_call_target="tpu_custom_call" | custom-call | bytes 2097152 | tf_op jit(solution)/shard_map/place/pallas_call | solution.py:320
  118.8 1.7 %place.5.rest_0_ = f32[2,2,512,512]{3,2,1,0:T(8,128)} custom-call(s32[2]{0:T(128)S(1)} %copy-done.2, f32[2,2,256,128]{3,2,1,0:T(8,128)S(1)} %collective-permute-done.7.even_ref, f32[2,2,256,128]{3,2,1,0:T(8,128)S(1)} %collective-permute-done.8.odd_ref, f32[2,2,512,512]{3,2,1,0:T(8,128)} %place.4.rest_0_), custom_call_target="tpu_custom_call", output_to_operand_aliasing={{}: (3, {})} | custom-call | bytes 2097152 | tf_op jit(solution)/shard_map/place/pallas_call | solution.py:320
  120.6 9.2 %collective-permute-done.6.odd_ref = f32[2,2,256,128]{3,2,1,0:T(8,128)S(1)} collective-permute-done((f32[2,2,256,128]{3,2,1,0:T(8,128)S(1)}, f32[2,2,256,128]{3,2,1,0:T(8,128)S(1)}, u32[]{:S(2)}, u32[]{:S(2)}) %collective-permute-start.6) | collective-permute-done | bytes 524320 | tf_op jit(solution)/shard_map/ppermute | solution.py:381
  129.8 1.7 %place.6.rest_0_ = f32[2,2,512,512]{3,2,1,0:T(8,128)} custom-call(s32[2]{0:T(128)S(1)} %copy-done.2, f32[2,2,256,128]{3,2,1,0:T(8,128)S(1)} %get-tuple-element.28.even_ref, f32[2,2,256,128]{3,2,1,0:T(8,128)S(1)} %collective-permute-done.6.odd_ref, f32[2,2,512,512]{3,2,1,0:T(8,128)} %place.5.rest_0_), custom_call_target="tpu_custom_call", output_to_operand_aliasing={{}: (3, {})} | custom-call | bytes 2097152 | tf_op jit(solution)/shard_map/place/pallas_call | solution.py:320
  131.5 7.3 %collective-permute-done.5.odd_ref = f32[2,2,256,128]{3,2,1,0:T(8,128)S(1)} collective-permute-done((f32[2,2,256,128]{3,2,1,0:T(8,128)S(1)}, f32[2,2,256,128]{3,2,1,0:T(8,128)S(1)}, u32[]{:S(2)}, u32[]{:S(2)}) %collective-permute-start.5) | collective-permute-done | bytes 524320 | tf_op jit(solution)/shard_map/ppermute | solution.py:381
  138.8 1.7 %place.7 = f32[2,2,512,512]{3,2,1,0:T(8,128)} custom-call(s32[2]{0:T(128)S(1)} %copy-done.2, f32[2,2,256,128]{3,2,1,0:T(8,128)S(1)} %collective-permute-done.4.even_ref, f32[2,2,256,128]{3,2,1,0:T(8,128)S(1)} %collective-permute-done.5.odd_ref, f32[2,2,512,512]{3,2,1,0:T(8,128)} %place.6.rest_0_), custom_call_target="tpu_custom_call", output_to_operand_aliasing={{}: (3, {})} | custom-call | bytes 2097152 | tf_op jit(solution)/shard_map/place/pallas_call | solution.py:320
  (21 shorter events, 1.4 us)
Async XLA Ops:
  4.1 59.1 %copy-start.5 = (f32[32,256]{1,0:T(8,128)S(1)}, f32[32,256]{1,0:T(8,128)}, u32[]{:S(2)}) copy-start(f32[32,256]{1,0:T(8,128)} %constant.28.clone) | copy-start | bytes 98308
  4.1 55.5 %all-to-all-start = ((f32[8,512,128]{2,1,0:T(8,128)}), f32[8,512,128]{2,1,0:T(8,128)S(1)}, u32[]{:S(2)}, u32[]{:S(2)}) async-start(f32[8,512,128]{2,1,0:T(8,128)} %bitcast.9), calls=%async_computation | async-start | bytes 4194304 | tf_op jit(solution)/shard_map/all_to_all | solution.py:359
  11.3 52.9 %copy-start = (bf16[512,256]{1,0:T(8,128)(2,1)S(1)}, bf16[512,256]{1,0:T(8,128)(2,1)}, u32[]{:S(2)}) copy-start(bf16[512,256]{1,0:T(8,128)(2,1)} %constant.30.clone.low_ref) | copy-start | bytes 786436
  11.3 53.0 %copy-start.2 = (s32[2]{0:T(128)S(1)}, s32[2]{0:T(128)}, u32[]{:S(2)}) copy-start(s32[2]{0:T(128)} %pad_add_fusion.meta_ref) | copy-start | bytes 28
  11.3 53.0 %copy-start.3 = (s32[512]{0:T(512)S(1)}, s32[512]{0:T(512)}, u32[]{:S(2)}) copy-start(s32[512]{0:T(512)} %param.7) | copy-start | bytes 6148
  11.4 53.0 %copy-start.4 = (s32[512]{0:T(512)S(1)}, s32[512]{0:T(512)}, u32[]{:S(2)}) copy-start(s32[512]{0:T(512)} %param.8) | copy-start | bytes 6148
  14.6 20.7 %collective-permute-start = (f32[1,512,128]{2,1,0:T(8,128)}, f32[1,512,128]{2,1,0:T(8,128)S(1)}, u32[]{:S(2)}, u32[]{:S(2)}) collective-permute-start(f32[1,512,128]{2,1,0:T(8,128)} %get-tuple-element.22), channel_id=1, source_target_pairs={{0,4},{4,0},{8,12},{12,8},{16,20},{20,16},{24,28},{28,24},{1,5},{5... | collective-permute-start | bytes 786440 | tf_op jit(solution)/shard_map/ppermute | solution.py:354
  16.6 36.5 %collective-permute-start.1 = (f32[1,512,128]{2,1,0:T(8,128)}, f32[1,512,128]{2,1,0:T(8,128)S(1)}, u32[]{:S(2)}, u32[]{:S(2)}) collective-permute-start(f32[1,512,128]{2,1,0:T(8,128)} %get-tuple-element.23), channel_id=1, source_target_pairs={{0,8},{4,12},{8,0},{12,4},{16,24},{20,28},{24,16},{28,20},{1,9},{5... | collective-permute-start | bytes 786440 | tf_op jit(solution)/shard_map/ppermute | solution.py:354
  18.1 39.5 %collective-permute-start.2 = (f32[1,512,128]{2,1,0:T(8,128)}, f32[1,512,128]{2,1,0:T(8,128)S(1)}, u32[]{:S(2)}, u32[]{:S(2)}) collective-permute-start(f32[1,512,128]{2,1,0:T(8,128)} %get-tuple-element.24), channel_id=1, source_target_pairs={{0,12},{4,8},{8,4},{12,0},{16,28},{20,24},{24,20},{28,16},{1,13},{... | collective-permute-start | bytes 786440 | tf_op jit(solution)/shard_map/ppermute | solution.py:354
  59.6 4.7 %copy-start.1 = (bf16[512,256]{1,0:T(8,128)(2,1)S(1)}, bf16[512,256]{1,0:T(8,128)(2,1)}, u32[]{:S(2)}) copy-start(bf16[512,256]{1,0:T(8,128)(2,1)} %constant.29.clone.high_ref) | copy-start | bytes 786436
  59.6 48.1 %collective-permute-start.3 = (f32[4,512,128]{2,1,0:T(8,128)S(1)}, f32[4,512,128]{2,1,0:T(8,128)S(1)}, u32[]{:S(2)}, u32[]{:S(2)}) collective-permute-start(f32[4,512,128]{2,1,0:T(8,128)S(1)} %pad_maximum_fusion.rest_0_), channel_id=1, source_target_pairs={{0,16},{4,20},{8,24},{12,28},{16,0},{20,4},{24,8},{28,12},{1,17},{... | collective-permute-start | bytes 3145736 | tf_op jit(solution)/shard_map/ppermute | solution.py:354
  70.1 44.5 %collective-permute-start.9 = (f32[2,2,256,128]{3,2,1,0:T(8,128)S(1)}, f32[2,2,256,128]{3,2,1,0:T(8,128)S(1)}, u32[]{:S(2)}, u32[]{:S(2)}) collective-permute-start(f32[2,2,256,128]{3,2,1,0:T(8,128)S(1)} %get-tuple-element.34), channel_id=1, source_target_pairs={{0,4},{4,0},{8,12},{12,8},{16,20},{20,16},{24,28},{28,24},{1,5},{5... | collective-permute-start | bytes 1572872 | tf_op jit(solution)/shard_map/ppermute | solution.py:381
  70.7 48.1 %collective-permute-start.7 = (f32[2,2,256,128]{3,2,1,0:T(8,128)S(1)}, f32[2,2,256,128]{3,2,1,0:T(8,128)S(1)}, u32[]{:S(2)}, u32[]{:S(2)}) collective-permute-start(f32[2,2,256,128]{3,2,1,0:T(8,128)S(1)} %get-tuple-element.31), channel_id=1, source_target_pairs={{0,8},{4,12},{8,0},{12,4},{16,24},{20,28},{24,16},{28,20},{1,9},{5... | collective-permute-start | bytes 1572872 | tf_op jit(solution)/shard_map/ppermute | solution.py:381
  70.7 48.1 %collective-permute-start.8 = (f32[2,2,256,128]{3,2,1,0:T(8,128)S(1)}, f32[2,2,256,128]{3,2,1,0:T(8,128)S(1)}, u32[]{:S(2)}, u32[]{:S(2)}) collective-permute-start(f32[2,2,256,128]{3,2,1,0:T(8,128)S(1)} %get-tuple-element.32), channel_id=1, source_target_pairs={{0,12},{4,8},{8,4},{12,0},{16,28},{20,24},{24,20},{28,16},{1,13},{... | collective-permute-start | bytes 1572872 | tf_op jit(solution)/shard_map/ppermute | solution.py:381
  113.6 16.3 %collective-permute-start.6 = (f32[2,2,256,128]{3,2,1,0:T(8,128)S(1)}, f32[2,2,256,128]{3,2,1,0:T(8,128)S(1)}, u32[]{:S(2)}, u32[]{:S(2)}) collective-permute-start(f32[2,2,256,128]{3,2,1,0:T(8,128)S(1)} %get-tuple-element.29), channel_id=1, source_target_pairs={{0,4},{4,0},{8,12},{12,8},{16,20},{20,16},{24,28},{28,24},{1,5},{5... | collective-permute-start | bytes 1572872 | tf_op jit(solution)/shard_map/ppermute | solution.py:381
  114.5 17.0 %collective-permute-start.4 = (f32[2,2,256,128]{3,2,1,0:T(8,128)S(1)}, f32[2,2,256,128]{3,2,1,0:T(8,128)S(1)}, u32[]{:S(2)}, u32[]{:S(2)}) collective-permute-start(f32[2,2,256,128]{3,2,1,0:T(8,128)S(1)} %get-tuple-element.26), channel_id=1, source_target_pairs={{0,8},{4,12},{8,0},{12,4},{16,24},{20,28},{24,16},{28,20},{1,9},{5... | collective-permute-start | bytes 1572872 | tf_op jit(solution)/shard_map/ppermute | solution.py:381
  114.5 24.2 %collective-permute-start.5 = (f32[2,2,256,128]{3,2,1,0:T(8,128)S(1)}, f32[2,2,256,128]{3,2,1,0:T(8,128)S(1)}, u32[]{:S(2)}, u32[]{:S(2)}) collective-permute-start(f32[2,2,256,128]{3,2,1,0:T(8,128)S(1)} %get-tuple-element.27), channel_id=1, source_target_pairs={{0,12},{4,8},{8,4},{12,0},{16,28},{20,24},{24,20},{28,16},{1,13},{... | collective-permute-start | bytes 1572872 | tf_op jit(solution)/shard_map/ppermute | solution.py:381

commit v2 on v1

--- a/solution.py
+++ b/solution.py
@@ -38,8 +38,9 @@
     return pltpu.roll(value, HALF_LANES, value.ndim - 1)
 
 
-def pack_kernel(meta_ref, in_hbm, *rest, side_size, plan):
-    outs, (lines, mixed, sems) = rest[:-3], rest[-3:]
+def pack_kernel(*refs, side_size, plan):
+    meta_ref, in_hbm = refs[0], refs[-len(plan) - 4]
+    outs, (lines, mixed, sems) = refs[-len(plan) - 3 : -3], refs[-3:]
     tiles = side_size // 2
     chunks = sorted({chunk for targets in plan for _, chunk, _, _ in targets})
     loads = {}
@@ -82,9 +83,10 @@
     hbm = pl.BlockSpec(memory_space=pl.ANY)
     chunks = len({chunk for targets in plan for _, chunk, _, _ in targets})
     copies = sum(len(targets) for targets in plan)
+    relative = any(target[3] for targets in plan for target in targets)
     return pl.pallas_call(
         functools.partial(pack_kernel, side_size=side_size, plan=plan),
-        in_specs=[pl.BlockSpec(memory_space=pltpu.SMEM), hbm],
+        in_specs=[pl.BlockSpec(memory_space=pltpu.SMEM)] * relative + [hbm],
         out_specs=[hbm] * len(plan),
         out_shape=[
             jax.ShapeDtypeStruct((*shape, block_len, LANES), jnp.float32) for shape in shapes
@@ -100,7 +102,7 @@
             bytes_accessed=4 * block_len * LANES * (chunks * side_size + copies),
         ),
         name="pack_lines",
-    )(meta, packed)
+    )(*[meta] * relative, packed)
 
 
 def add(left, right):
@@ -132,50 +134,80 @@
     return [add(e, o) for e, o in zip(even, odd)] + [sub(e, o) for e, o in zip(even, odd)]
 
 
-def transform_kernel(
-    meta_ref, wave_y_ref, wave_z_ref, high_ref, low_ref, twiddle_hbm, *rest, chunk, side_size, spots
-):
-    operands = 1 + max(operand for operand, _, _, _ in spots)
-    inputs, rest = rest[:operands], rest[operands:]
-    outs = rest[:side_size]
-    split_high, split_low, product, result, twiddle, line, sems, line_sems = rest[side_size:]
-    block_len = inputs[0].shape[-2]
-    span = block_len // RADIX
-    device_pos = meta_ref[1] * side_size + meta_ref[0]
-    per_owner = HALF_RADIX // side_size
-    load = pltpu.make_async_copy(twiddle_hbm, twiddle, sems.at[side_size])
-    load.start()
-    fetches, targets = [], []
-    for step, (operand, spot, place, relative) in enumerate(spots):
-        rows = pl.ds(place * span, span)
-        if relative:
-            source = lax.bitwise_xor(device_pos, place)
-            fetches.append(
-                pltpu.make_async_copy(
-                    inputs[operand].at[spot], line.at[source], line_sems.at[step]
-                )
-            )
-            fetches[-1].start()
-            targets.append((line, place, rows))
-        else:
-            targets.append((inputs[operand], spot, rows))
-    for fetch in fetches:
-        fetch.wait()
+def contract(matrices, start, depth, blocks, split_high, split_low, store):
+    span = depth // len(blocks)
+    high, low = (ref[:, pl.ds(start, depth)] for ref in matrices)
     dot = functools.partial(jnp.dot, preferred_element_type=jnp.float32)
     for pair in range(RADIX // 2):
         columns = slice(2 * pair * LANES, 2 * (pair + 1) * LANES)
         for digit in (2 * pair, 2 * pair + 1):
             own = slice(digit * LANES, (digit + 1) * LANES)
-            for ref, spot, rows in targets:
-                value = ref[spot, pl.ds(digit, span, stride=RADIX), :]
-                high = value.astype(jnp.bfloat16)
-                split_high[rows, own] = high
-                split_low[rows, own] = (value - high.astype(jnp.float32)).astype(jnp.bfloat16)
-        product[:, columns] = (
-            dot(high_ref[...], split_high[:, columns])
-            + dot(high_ref[...], split_low[:, columns])
-            + dot(low_ref[...], split_high[:, columns])
-        )
+            for place, (ref, index) in enumerate(blocks):
+                rows = slice(place * span, (place + 1) * span)
+                value = ref[index, pl.ds(digit, span, stride=RADIX), :]
+                top = value.astype(jnp.bfloat16)
+                split_high[rows, own] = top
+                split_low[rows, own] = (value - top.astype(jnp.float32)).astype(jnp.bfloat16)
+        total = dot(high, split_high[:, columns]) + dot(high, split_low[:, columns])
+        store(columns, total + dot(low, split_high[:, columns]))
+
+
+def begin_kernel(meta_ref, high_ref, low_ref, near_ref, out_ref, split_high, split_low):
+    side_size = near_ref.shape[0]
+    depth = SUB // 2
+    start = pl.multiple_of(meta_ref[1] * depth, depth)
+    blocks = [(near_ref, lax.bitwise_xor(meta_ref[0], place)) for place in range(side_size)]
+
+    def store(columns, value):
+        out_ref[:, columns] = value
+
+    contract((high_ref, low_ref), start, depth, blocks, split_high, split_low, store)
+
+
+def begin(meta, tables, near):
+    vmem = pl.BlockSpec(memory_space=pltpu.VMEM)
+    return pl.pallas_call(
+        begin_kernel,
+        in_specs=[pl.BlockSpec(memory_space=pltpu.SMEM)] + [vmem] * 3,
+        out_specs=vmem,
+        out_shape=jax.ShapeDtypeStruct((2 * SUB, RADIX * LANES), jnp.float32),
+        scratch_shapes=[pltpu.VMEM((SUB // 2, RADIX * LANES), jnp.bfloat16)] * 2,
+        compiler_params=pltpu.CompilerParams(vmem_limit_bytes=16 * MIB),
+        cost_estimate=pl.CostEstimate(
+            flops=6 * SUB * SUB * RADIX * LANES, transcendentals=0, bytes_accessed=5 * MIB
+        ),
+        name="begin",
+    )(meta, *tables[:2], near)
+
+
+def transform_kernel(
+    meta_ref, wave_y_ref, wave_z_ref, high_ref, low_ref, twiddle, *rest, chunk, side_size, begun
+):
+    count = 3 if begun else 1
+    inputs, rest = rest[:count], rest[count:]
+    outs = rest[:side_size]
+    split_high, split_low, product, result, line, sems, line_sems = rest[side_size:]
+    per_owner = HALF_RADIX // side_size
+    if begun:
+        depth = SUB // 2
+        start = pl.multiple_of((1 - meta_ref[1]) * depth, depth)
+        fetches = []
+        for step in range(side_size):
+            ref = inputs[2].at[step - 1] if step else inputs[1].at[0]
+            spot = line.at[lax.bitwise_xor(meta_ref[0], step)]
+            fetches.append(pltpu.make_async_copy(ref, spot, line_sems.at[step]))
+            fetches[-1].start()
+        for fetch in fetches:
+            fetch.wait()
+        blocks = [(line, place) for place in range(side_size)]
+    else:
+        depth, start = SUB, 0
+        blocks = [(inputs[0], place) for place in range(2 * side_size)]
+
+    def store(columns, value):
+        product[:, columns] = inputs[0][:, columns] + value if begun else value
+
+    contract((high_ref, low_ref), start, depth, blocks, split_high, split_low, store)
 
     own_place = meta_ref[0]
     side_float = meta_ref[1].astype(jnp.float32)
@@ -192,7 +224,6 @@
     along_y = jnp.broadcast_to(own_y, (8, LANES))
     cross = jnp.broadcast_to(own_y * own_y + own_z * own_z, (8, LANES))
     row_ids = lax.broadcasted_iota(jnp.int32, (8, LANES), 0).astype(jnp.float32) - 2048.0 * side_float
-    load.wait()
 
     def rows_body(step, carry):
         start = pl.multiple_of(step * 8, 8)
@@ -229,7 +260,7 @@
     parts = 2
     for part in range(parts):
         steps = SUB // 8 // parts
-        lax.fori_loop(part * steps, (part + 1) * steps, rows_body, 0, unroll=UNROLL)
+        lax.fori_loop(part * steps, (part + 1) * steps, rows_body, 0, unroll=4)
         rows = pl.ds(part * SUB // parts, SUB // parts)
         for step in range(side_size):
             owner = lax.bitwise_xor(own_place, step)
@@ -245,28 +276,26 @@
         copy.wait()
 
 
-UNROLL = 4
-
-
-def transform(meta, wave_y, wave_z, tables, arrays, spots, chunk, side_size):
+def transform(meta, wave_y, wave_z, tables, arrays, chunk, side_size):
     per_owner = HALF_RADIX // side_size
+    begun = len(arrays) == 3
+    depth = SUB // 2 if begun else SUB
     vmem = pl.BlockSpec(memory_space=pltpu.VMEM)
     hbm = pl.BlockSpec(memory_space=pl.ANY)
     block = jax.ShapeDtypeStruct((per_owner, 2, SUB, LANES), jnp.float32)
     return pl.pallas_call(
-        functools.partial(transform_kernel, chunk=chunk, side_size=side_size, spots=spots),
-        in_specs=[pl.BlockSpec(memory_space=pltpu.SMEM)] + [vmem] * 4 + [hbm] + [vmem] * len(arrays),
+        functools.partial(transform_kernel, chunk=chunk, side_size=side_size, begun=begun),
+        in_specs=[pl.BlockSpec(memory_space=pltpu.SMEM)] + [vmem] * (5 + len(arrays)),
         out_specs=[hbm] * side_size,
         out_shape=[block] * side_size,
         scratch_shapes=[
-            pltpu.VMEM((SUB, RADIX * LANES), jnp.bfloat16),
-            pltpu.VMEM((SUB, RADIX * LANES), jnp.bfloat16),
+            pltpu.VMEM((depth, RADIX * LANES), jnp.bfloat16),
+            pltpu.VMEM((depth, RADIX * LANES), jnp.bfloat16),
             pltpu.VMEM((2 * SUB, RADIX * LANES), jnp.float32),
             pltpu.VMEM((HALF_RADIX, 2, SUB, LANES), jnp.float32),
-            pltpu.VMEM((2 * RADIX, SUB, LANES), jnp.float32),
-            pltpu.VMEM((2 * side_size, NX // (2 * side_size), LANES), jnp.float32),
+            pltpu.VMEM((side_size, NX // (2 * side_size), LANES), jnp.float32),
             pltpu.SemaphoreType.DMA((2 * side_size + 1,)),
-            pltpu.SemaphoreType.DMA((2 * side_size,)),
+            pltpu.SemaphoreType.DMA((side_size,)),
         ],
         compiler_params=pltpu.CompilerParams(vmem_limit_bytes=24 * MIB),
         cost_estimate=pl.CostEstimate(
@@ -359,22 +388,21 @@
     got = lax.all_to_all(
         send.reshape(cycle_size, block_len, LANES), "gx", split_axis=0, concat_axis=0, tiled=True
     )
-    lines = [([got], [(0, place, place, False) for place in range(cycle_size)])]
+    lines = [[got]]
     for chunk in range(1, chunks):
         (send,), packed = lax.optimization_barrier(((send,), packed))
         near_plan = [[(0, chunk, place, True)] for place in places]
-        near = pack_lines(meta, packed, side_size, near_plan, [(1,)] * side_size)
-        near = [near[0]] + [swap(near[place], place) for place in places[1:]]
-        held = jnp.concatenate(near)
-        got, held = lax.optimization_barrier((got, held))
-        lines[0] = ([got], lines[0][1])
-        far = swap(held, side_size)
-        spots = [(0, place, place, True) for place in places]
-        spots += [(1, place, side_size + place, True) for place in places]
-        lines.append(([held, far], spots))
+        sends = pack_lines(meta, packed, side_size, near_plan, [(1,)] * side_size)
+        early = swap(sends[0], side_size)
+        near = [swap(sends[place], place) for place in places[1:]]
+        others = jnp.concatenate(near)
+        got, others = lax.optimization_barrier((got, others))
+        lines[0] = [got]
+        held = jnp.concatenate([sends[0], others])
+        lines.append([begin(meta, tables, held), early, swap(others, side_size)])
     result = None
     for chunk in range(chunks):
-        blocks = transform(meta, wave_y, wave_z, tables, *lines[chunk], chunk, side_size)
+        blocks = transform(meta, wave_y, wave_z, tables, lines[chunk], chunk, side_size)
         blocks = [
             block
             if step == 0

time: 141 us -> 139 us (0.986)
    ppermute x4 -> x5, waiting for transfers between devices: 73.6 us -> 70.4 us  [swap(): return lax.ppermute(value, 'gx', [(i, i ^ step) for i in range(cycle_size)])]
    pallas_call x0 -> x1, Pallas kernels: none -> 2.51 us  [begin(): pl.pallas_call(begin_kernel, in_specs=[pl.BlockSpec(memory_space=pltpu.SM...]
    ppermute x4 -> x5, starting transfers between devices: 7.17 us -> 7.42 us  [swap(): return lax.ppermute(value, 'gx', [(i, i ^ step) for i in range(cycle_size)])]
  transfers between devices with their start and end apart: 11 -> 12, of which waited for: 7 -> 7; matrix products, arithmetic and copies ran while one was open for 2% -> 1% of each run, Pallas kernels for 14% -> 15%
where the time goes in v2:
time: 139 us
  waiting for transfers between devices  90.1 us (65%)
  Pallas kernels  25.8 us (19%)
  starting transfers between devices  20.9 us (15%)
    ppermute x5, waiting for transfers between devices, swap(): return lax.ppermute(value, 'gx', [(i, i ^ step) for i in range(cycle_size)])  70.4 us
    ppermute x6, waiting for transfers between devices, shards(): lax.ppermute(block, 'gx', [(i, i ^ step) for i in range(cycle_size)])  17.9 us
    pallas_call x2, Pallas kernels, transform(): pl.pallas_call(functools.partial(transform_kernel, chunk=chunk, side_size...  10.5 us
    ppermute x5, starting transfers between devices, swap(): return lax.ppermute(value, 'gx', [(i, i ^ step) for i in range(cycle_size)])  7.42 us
    all_to_all x1, starting transfers between devices, shards(): lax.all_to_all(send.reshape(cycle_size, block_len, LANES), 'gx', split_ax...  7.26 us
    pallas_call x4, Pallas kernels, place(): pl.pallas_call(functools.partial(place_kernel, chunk=chunk, step=step, si...  6.81 us
    ppermute x6, starting transfers between devices, shards(): lax.ppermute(block, 'gx', [(i, i ^ step) for i in range(cycle_size)])  6.22 us
    pallas_call x2, Pallas kernels, pack_lines(): pl.pallas_call(functools.partial(pack_kernel, side_size=side_size, plan=p...  5.92 us
  transfers between devices with their start and end apart: 12, of which 7 were waited for; matrix products, arithmetic and copies ran while one was open for 1% of the time, Pallas kernels for 15%

profile of v2, /device:TPU:0, one launch (start us, length us, event | category | flops | bytes accessed | tf_op | source)
XLA Modules:
  0.0 138.9 jit_solution(2338572882855867573)
XLA Ops:
  0.0 2.7 %pack_lines.2 = f32[2,4,512,128]{3,2,1,0:T(8,128)} custom-call(f32[2,512,512]{2,1,0:T(8,128)} %refs_1_), custom_call_target="tpu_custom_call" | custom-call | bytes 3145728 | tf_op jit(solution)/shard_map/pack_lines/pallas_call | solution.py:87
  2.8 7.3 %all-to-all-start = ((f32[8,512,128]{2,1,0:T(8,128)}), f32[8,512,128]{2,1,0:T(8,128)S(1)}, u32[]{:S(2)}, u32[]{:S(2)}) async-start(f32[8,512,128]{2,1,0:T(8,128)} %bitcast.9), calls=%async_computation | async-start | bytes 4194304 | tf_op jit(solution)/shard_map/all_to_all | solution.py:388
  10.7 3.2 %pack_lines.3 = (f32[1,512,128]{2,1,0:T(8,128)}, f32[1,512,128]{2,1,0:T(8,128)}, f32[1,512,128]{2,1,0:T(8,128)}, f32[1,512,128]{2,1,0:T(8,128)}) custom-call(s32[2]{0:T(128)} %pad_add_fusion.refs_0_.meta_ref, f32[2,512,512]{2,1,0:T(8,128)} %refs_1_), custom_call_target="tpu_custom_call" | custom-call | bytes 2097152 | tf_op jit(solution)/shard_map/pack_lines/pallas_call | solution.py:87
  13.9 2.1 %collective-permute-start = (f32[1,512,128]{2,1,0:T(8,128)}, f32[1,512,128]{2,1,0:T(8,128)S(1)}, u32[]{:S(2)}, u32[]{:S(2)}) collective-permute-start(f32[1,512,128]{2,1,0:T(8,128)} %get-tuple-element.22), channel_id=1, source_target_pairs={{0,4},{4,0},{8,12},{12,8},{16,20},{20,16},{24,28},{28,24},{1,5},{5... | collective-permute-start | bytes 786440 | tf_op jit(solution)/shard_map/ppermute | solution.py:383
  16.0 1.5 %collective-permute-start.1 = (f32[1,512,128]{2,1,0:T(8,128)}, f32[1,512,128]{2,1,0:T(8,128)S(1)}, u32[]{:S(2)}, u32[]{:S(2)}) collective-permute-start(f32[1,512,128]{2,1,0:T(8,128)} %get-tuple-element.23), channel_id=1, source_target_pairs={{0,8},{4,12},{8,0},{12,4},{16,24},{20,28},{24,16},{28,20},{1,9},{5... | collective-permute-start | bytes 786440 | tf_op jit(solution)/shard_map/ppermute | solution.py:383
  17.5 16.5 %collective-permute-done = f32[1,512,128]{2,1,0:T(8,128)S(1)} collective-permute-done((f32[1,512,128]{2,1,0:T(8,128)}, f32[1,512,128]{2,1,0:T(8,128)S(1)}, u32[]{:S(2)}, u32[]{:S(2)}) %collective-permute-start) | collective-permute-done | bytes 262176 | tf_op jit(solution)/shard_map/ppermute | solution.py:383
  34.0 17.9 %collective-permute-done.1 = f32[1,512,128]{2,1,0:T(8,128)S(1)} collective-permute-done((f32[1,512,128]{2,1,0:T(8,128)}, f32[1,512,128]{2,1,0:T(8,128)S(1)}, u32[]{:S(2)}, u32[]{:S(2)}) %collective-permute-start.1) | collective-permute-done | bytes 262176 | tf_op jit(solution)/shard_map/ppermute | solution.py:383
  51.9 4.5 %collective-permute-done.2 = f32[1,512,128]{2,1,0:T(8,128)S(1)} collective-permute-done((f32[1,512,128]{2,1,0:T(8,128)}, f32[1,512,128]{2,1,0:T(8,128)S(1)}, u32[]{:S(2)}, u32[]{:S(2)}) %collective-permute-start.2) | collective-permute-done | bytes 262176 | tf_op jit(solution)/shard_map/ppermute | solution.py:383
  56.4 1.9 %all-to-all-done.rest_0_ = f32[8,512,128]{2,1,0:T(8,128)S(1)} async-done(((f32[8,512,128]{2,1,0:T(8,128)}), f32[8,512,128]{2,1,0:T(8,128)S(1)}, u32[]{:S(2)}, u32[]{:S(2)}) %all-to-all-start) | async-done | bytes 2097184 | tf_op jit(solution)/shard_map/all_to_all | solution.py:388
  58.3 2.6 %collective-permute-start.4 = (f32[3,512,128]{2,1,0:T(8,128)S(1)}, f32[3,512,128]{2,1,0:T(8,128)S(1)}, u32[]{:S(2)}, u32[]{:S(2)}) collective-permute-start(f32[3,512,128]{2,1,0:T(8,128)S(1)} %pad_maximum_fusion.1), channel_id=1, source_target_pairs={{0,16},{4,20},{8,24},{12,28},{16,0},{20,4},{24,8},{28,12},{1,17},{... | collective-permute-start | bytes 2359304 | tf_op jit(solution)/shard_map/ppermute | solution.py:383
  62.0 5.4 %transform.3 = (f32[2,2,256,128]{3,2,1,0:T(8,128)S(1)}, f32[2,2,256,128]{3,2,1,0:T(8,128)S(1)}, f32[2,2,256,128]{3,2,1,0:T(8,128)S(1)}, f32[2,2,256,128]{3,2,1,0:T(8,128)S(1)}) custom-call(s32[2]{0:T(128)S(1)} %copy-done.2, s32[4,128]{1,0:T(4,128)S(1)} %bitcast.5, s32[4,128]{1,0:T(4,128)S(1)} %bitcast.7, bf16[512,256]{1,0:T(8,128)(2,1)S(1)} %copy-done.1, ...), custom_call_target="tpu_custom_call" | custom-call | flops 1610612736 | bytes 5242880 | tf_op jit(solution)/shard_map/transform/pallas_call | solution.py:286
  68.1 1.2 collective-permute-start.3
  69.9 1.4 %collective-permute-start.9 = (f32[2,2,256,128]{3,2,1,0:T(8,128)S(1)}, f32[2,2,256,128]{3,2,1,0:T(8,128)S(1)}, u32[]{:S(2)}, u32[]{:S(2)}) collective-permute-start(f32[2,2,256,128]{3,2,1,0:T(8,128)S(1)} %get-tuple-element.32), channel_id=1, source_target_pairs={{0,12},{4,8},{8,4},{12,0},{16,28},{20,24},{24,20},{28,16},{1,13},{... | collective-permute-start | bytes 1572872 | tf_op jit(solution)/shard_map/ppermute | solution.py:409
  71.4 2.5 %begin.1.rest_0_ = f32[512,2048]{1,0:T(8,128)S(1)} custom-call(s32[2]{0:T(128)S(1)} %copy-done.2, bf16[512,256]{1,0:T(8,128)(2,1)S(1)} %copy-done.1, bf16[512,256]{1,0:T(8,128)(2,1)S(1)} %copy-done, f32[4,512,128]{2,1,0:T(8,128)S(1)} %pad_maximum_fusion.near_ref), custom_call_target="tpu_custom_call" | custom-call | flops 805306368 | bytes 5242880 | tf_op jit(solution)/shard_map/begin/pallas_call | solution.py:169
  73.9 31.6 %collective-permute-done.3.rest_1_ = f32[1,512,128]{2,1,0:T(8,128)S(1)} collective-permute-done((f32[1,512,128]{2,1,0:T(8,128)S(1)}, f32[1,512,128]{2,1,0:T(8,128)S(1)}, u32[]{:S(2)}, u32[]{:S(2)}) %collective-permute-start.3) | collective-permute-done | bytes 262176 | tf_op jit(solution)/shard_map/ppermute | solution.py:383
  105.5 5.2 %transform.2 = (f32[2,2,256,128]{3,2,1,0:T(8,128)S(1)}, f32[2,2,256,128]{3,2,1,0:T(8,128)S(1)}, f32[2,2,256,128]{3,2,1,0:T(8,128)S(1)}, f32[2,2,256,128]{3,2,1,0:T(8,128)S(1)}) custom-call(s32[2]{0:T(128)S(1)} %copy-done.2, s32[4,128]{1,0:T(4,128)S(1)} %bitcast.6, s32[4,128]{1,0:T(4,128)S(1)} %bitcast.8, bf16[512,256]{1,0:T(8,128)(2,1)S(1)} %copy-done.1, ...), custom_call_target="tpu_custom_call" | custom-call | flops 1610612736 | bytes 5242880 | tf_op jit(solution)/shard_map/transform/pallas_call | solution.py:286
  110.7 1.8 %collective-permute-start.7 = (f32[2,2,256,128]{3,2,1,0:T(8,128)S(1)}, f32[2,2,256,128]{3,2,1,0:T(8,128)S(1)}, u32[]{:S(2)}, u32[]{:S(2)}) collective-permute-start(f32[2,2,256,128]{3,2,1,0:T(8,128)S(1)} %get-tuple-element.29), channel_id=1, source_target_pairs={{0,4},{4,0},{8,12},{12,8},{16,20},{20,16},{24,28},{28,24},{1,5},{5... | collective-permute-start | bytes 1572872 | tf_op jit(solution)/shard_map/ppermute | solution.py:409
  112.5 1.7 %collective-permute-start.6 = (f32[2,2,256,128]{3,2,1,0:T(8,128)S(1)}, f32[2,2,256,128]{3,2,1,0:T(8,128)S(1)}, u32[]{:S(2)}, u32[]{:S(2)}) collective-permute-start(f32[2,2,256,128]{3,2,1,0:T(8,128)S(1)} %get-tuple-element.27), channel_id=1, source_target_pairs={{0,12},{4,8},{8,4},{12,0},{16,28},{20,24},{24,20},{28,16},{1,13},{... | collective-permute-start | bytes 1572872 | tf_op jit(solution)/shard_map/ppermute | solution.py:409
  114.2 1.7 %place.4.rest_0_ = f32[2,2,512,512]{3,2,1,0:T(8,128)} custom-call(s32[2]{0:T(128)S(1)} %copy-done.2, f32[2,2,256,128]{3,2,1,0:T(8,128)S(1)} %get-tuple-element.33.even_ref, f32[2,2,256,128]{3,2,1,0:T(8,128)S(1)} %collective-permute-done.10.odd_ref), custom_call_target="tpu_custom_call" | custom-call | bytes 2097152 | tf_op jit(solution)/shard_map/place/pallas_call | solution.py:349
  115.9 1.7 %place.5.rest_0_ = f32[2,2,512,512]{3,2,1,0:T(8,128)} custom-call(s32[2]{0:T(128)S(1)} %copy-done.2, f32[2,2,256,128]{3,2,1,0:T(8,128)S(1)} %collective-permute-done.8.even_ref, f32[2,2,256,128]{3,2,1,0:T(8,128)S(1)} %collective-permute-done.9.odd_ref, f32[2,2,512,512]{3,2,1,0:T(8,128)} %place.4.rest_0_), custom_call_target="tpu_custom_call", output_to_operand_aliasing={{}: (3, {})} | custom-call | bytes 2097152 | tf_op jit(solution)/shard_map/place/pallas_call | solution.py:349
  117.7 9.4 %collective-permute-done.7.odd_ref = f32[2,2,256,128]{3,2,1,0:T(8,128)S(1)} collective-permute-done((f32[2,2,256,128]{3,2,1,0:T(8,128)S(1)}, f32[2,2,256,128]{3,2,1,0:T(8,128)S(1)}, u32[]{:S(2)}, u32[]{:S(2)}) %collective-permute-start.7) | collective-permute-done | bytes 524320 | tf_op jit(solution)/shard_map/ppermute | solution.py:409
  127.0 1.7 %place.6.rest_0_ = f32[2,2,512,512]{3,2,1,0:T(8,128)} custom-call(s32[2]{0:T(128)S(1)} %copy-done.2, f32[2,2,256,128]{3,2,1,0:T(8,128)S(1)} %get-tuple-element.28.even_ref, f32[2,2,256,128]{3,2,1,0:T(8,128)S(1)} %collective-permute-done.7.odd_ref, f32[2,2,512,512]{3,2,1,0:T(8,128)} %place.5.rest_0_), custom_call_target="tpu_custom_call", output_to_operand_aliasing={{}: (3, {})} | custom-call | bytes 2097152 | tf_op jit(solution)/shard_map/place/pallas_call | solution.py:349
  128.7 8.5 %collective-permute-done.6.odd_ref = f32[2,2,256,128]{3,2,1,0:T(8,128)S(1)} collective-permute-done((f32[2,2,256,128]{3,2,1,0:T(8,128)S(1)}, f32[2,2,256,128]{3,2,1,0:T(8,128)S(1)}, u32[]{:S(2)}, u32[]{:S(2)}) %collective-permute-start.6) | collective-permute-done | bytes 524320 | tf_op jit(solution)/shard_map/ppermute | solution.py:409
  137.2 1.7 %place.7 = f32[2,2,512,512]{3,2,1,0:T(8,128)} custom-call(s32[2]{0:T(128)S(1)} %copy-done.2, f32[2,2,256,128]{3,2,1,0:T(8,128)S(1)} %collective-permute-done.5.even_ref, f32[2,2,256,128]{3,2,1,0:T(8,128)S(1)} %collective-permute-done.6.odd_ref, f32[2,2,512,512]{3,2,1,0:T(8,128)} %place.6.rest_0_), custom_call_target="tpu_custom_call", output_to_operand_aliasing={{}: (3, {})} | custom-call | bytes 2097152 | tf_op jit(solution)/shard_map/place/pallas_call | solution.py:349
  (27 shorter events, 3.3 us)
Async XLA Ops:
  2.7 58.1 %copy-start.6 = (f32[32,256]{1,0:T(8,128)S(1)}, f32[32,256]{1,0:T(8,128)}, u32[]{:S(2)}) copy-start(f32[32,256]{1,0:T(8,128)} %constant.28.clone) | copy-start | bytes 98308
  2.8 55.5 %all-to-all-start = ((f32[8,512,128]{2,1,0:T(8,128)}), f32[8,512,128]{2,1,0:T(8,128)S(1)}, u32[]{:S(2)}, u32[]{:S(2)}) async-start(f32[8,512,128]{2,1,0:T(8,128)} %bitcast.9), calls=%async_computation | async-start | bytes 4194304 | tf_op jit(solution)/shard_map/all_to_all | solution.py:388
  10.0 52.0 %copy-start = (bf16[512,256]{1,0:T(8,128)(2,1)S(1)}, bf16[512,256]{1,0:T(8,128)(2,1)}, u32[]{:S(2)}) copy-start(bf16[512,256]{1,0:T(8,128)(2,1)} %constant.30.clone.low_ref) | copy-start | bytes 786436
  10.0 52.0 %copy-start.1 = (bf16[512,256]{1,0:T(8,128)(2,1)S(1)}, bf16[512,256]{1,0:T(8,128)(2,1)}, u32[]{:S(2)}) copy-start(bf16[512,256]{1,0:T(8,128)(2,1)} %constant.29.clone.high_ref) | copy-start | bytes 786436
  10.0 52.0 %copy-start.3 = (s32[512]{0:T(512)S(1)}, s32[512]{0:T(512)}, u32[]{:S(2)}) copy-start(s32[512]{0:T(512)} %param.7) | copy-start | bytes 6148
  10.0 52.0 %copy-start.4 = (s32[512]{0:T(512)S(1)}, s32[512]{0:T(512)}, u32[]{:S(2)}) copy-start(s32[512]{0:T(512)} %param.8) | copy-start | bytes 6148
  10.7 51.3 %copy-start.2 = (s32[2]{0:T(128)S(1)}, s32[2]{0:T(128)}, u32[]{:S(2)}) copy-start(s32[2]{0:T(128)} %pad_add_fusion.refs_0_.meta_ref) | copy-start | bytes 28
  13.9 20.1 %collective-permute-start = (f32[1,512,128]{2,1,0:T(8,128)}, f32[1,512,128]{2,1,0:T(8,128)S(1)}, u32[]{:S(2)}, u32[]{:S(2)}) collective-permute-start(f32[1,512,128]{2,1,0:T(8,128)} %get-tuple-element.22), channel_id=1, source_target_pairs={{0,4},{4,0},{8,12},{12,8},{16,20},{20,16},{24,28},{28,24},{1,5},{5... | collective-permute-start | bytes 786440 | tf_op jit(solution)/shard_map/ppermute | solution.py:383
  16.0 35.9 %collective-permute-start.1 = (f32[1,512,128]{2,1,0:T(8,128)}, f32[1,512,128]{2,1,0:T(8,128)S(1)}, u32[]{:S(2)}, u32[]{:S(2)}) collective-permute-start(f32[1,512,128]{2,1,0:T(8,128)} %get-tuple-element.23), channel_id=1, source_target_pairs={{0,8},{4,12},{8,0},{12,4},{16,24},{20,28},{24,16},{28,20},{1,9},{5... | collective-permute-start | bytes 786440 | tf_op jit(solution)/shard_map/ppermute | solution.py:383
  17.5 38.9 %collective-permute-start.2 = (f32[1,512,128]{2,1,0:T(8,128)}, f32[1,512,128]{2,1,0:T(8,128)S(1)}, u32[]{:S(2)}, u32[]{:S(2)}) collective-permute-start(f32[1,512,128]{2,1,0:T(8,128)} %get-tuple-element.24), channel_id=1, source_target_pairs={{0,12},{4,8},{8,4},{12,0},{16,28},{20,24},{24,20},{28,16},{1,13},{... | collective-permute-start | bytes 786440 | tf_op jit(solution)/shard_map/ppermute | solution.py:383
  58.3 47.2 %collective-permute-start.4 = (f32[3,512,128]{2,1,0:T(8,128)S(1)}, f32[3,512,128]{2,1,0:T(8,128)S(1)}, u32[]{:S(2)}, u32[]{:S(2)}) collective-permute-start(f32[3,512,128]{2,1,0:T(8,128)S(1)} %pad_maximum_fusion.1), channel_id=1, source_target_pairs={{0,16},{4,20},{8,24},{12,28},{16,0},{20,4},{24,8},{28,12},{1,17},{... | collective-permute-start | bytes 2359304 | tf_op jit(solution)/shard_map/ppermute | solution.py:383
  62.0 6.0 %copy-start.5 = (f32[1,512,128]{2,1,0:T(8,128)S(1)}, f32[1,512,128]{2,1,0:T(8,128)}, u32[]{:S(2)}) copy-start(f32[1,512,128]{2,1,0:T(8,128)} %get-tuple-element.21) | copy-start | bytes 786436
  67.4 45.0 %collective-permute-start.10 = (f32[2,2,256,128]{3,2,1,0:T(8,128)S(1)}, f32[2,2,256,128]{3,2,1,0:T(8,128)S(1)}, u32[]{:S(2)}, u32[]{:S(2)}) collective-permute-start(f32[2,2,256,128]{3,2,1,0:T(8,128)S(1)} %get-tuple-element.34), channel_id=1, source_target_pairs={{0,4},{4,0},{8,12},{12,8},{16,20},{20,16},{24,28},{28,24},{1,5},{5... | collective-permute-start | bytes 1572872 | tf_op jit(solution)/shard_map/ppermute | solution.py:409
  68.1 37.4 %collective-permute-start.3 = (f32[1,512,128]{2,1,0:T(8,128)S(1)}, f32[1,512,128]{2,1,0:T(8,128)S(1)}, u32[]{:S(2)}, u32[]{:S(2)}) collective-permute-start(f32[1,512,128]{2,1,0:T(8,128)S(1)} %copy-done.5), channel_id=1, source_target_pairs={{0,16},{4,20},{8,24},{12,28},{16,0},{20,4},{24,8},{28,12},{1,17},{... | collective-permute-start | bytes 786440 | tf_op jit(solution)/shard_map/ppermute | solution.py:383
  69.3 46.6 %collective-permute-start.8 = (f32[2,2,256,128]{3,2,1,0:T(8,128)S(1)}, f32[2,2,256,128]{3,2,1,0:T(8,128)S(1)}, u32[]{:S(2)}, u32[]{:S(2)}) collective-permute-start(f32[2,2,256,128]{3,2,1,0:T(8,128)S(1)} %get-tuple-element.31), channel_id=1, source_target_pairs={{0,8},{4,12},{8,0},{12,4},{16,24},{20,28},{24,16},{28,20},{1,9},{5... | collective-permute-start | bytes 1572872 | tf_op jit(solution)/shard_map/ppermute | solution.py:409
  69.9 46.1 %collective-permute-start.9 = (f32[2,2,256,128]{3,2,1,0:T(8,128)S(1)}, f32[2,2,256,128]{3,2,1,0:T(8,128)S(1)}, u32[]{:S(2)}, u32[]{:S(2)}) collective-permute-start(f32[2,2,256,128]{3,2,1,0:T(8,128)S(1)} %get-tuple-element.32), channel_id=1, source_target_pairs={{0,12},{4,8},{8,4},{12,0},{16,28},{20,24},{24,20},{28,16},{1,13},{... | collective-permute-start | bytes 1572872 | tf_op jit(solution)/shard_map/ppermute | solution.py:409
  110.7 16.4 %collective-permute-start.7 = (f32[2,2,256,128]{3,2,1,0:T(8,128)S(1)}, f32[2,2,256,128]{3,2,1,0:T(8,128)S(1)}, u32[]{:S(2)}, u32[]{:S(2)}) collective-permute-start(f32[2,2,256,128]{3,2,1,0:T(8,128)S(1)} %get-tuple-element.29), channel_id=1, source_target_pairs={{0,4},{4,0},{8,12},{12,8},{16,20},{20,16},{24,28},{28,24},{1,5},{5... | collective-permute-start | bytes 1572872 | tf_op jit(solution)/shard_map/ppermute | solution.py:409
  112.5 16.2 %collective-permute-start.5 = (f32[2,2,256,128]{3,2,1,0:T(8,128)S(1)}, f32[2,2,256,128]{3,2,1,0:T(8,128)S(1)}, u32[]{:S(2)}, u32[]{:S(2)}) collective-permute-start(f32[2,2,256,128]{3,2,1,0:T(8,128)S(1)} %get-tuple-element.26), channel_id=1, source_target_pairs={{0,8},{4,12},{8,0},{12,4},{16,24},{20,28},{24,16},{28,20},{1,9},{5... | collective-permute-start | bytes 1572872 | tf_op jit(solution)/shard_map/ppermute | solution.py:409
  112.5 24.8 %collective-permute-start.6 = (f32[2,2,256,128]{3,2,1,0:T(8,128)S(1)}, f32[2,2,256,128]{3,2,1,0:T(8,128)S(1)}, u32[]{:S(2)}, u32[]{:S(2)}) collective-permute-start(f32[2,2,256,128]{3,2,1,0:T(8,128)S(1)} %get-tuple-element.27), channel_id=1, source_target_pairs={{0,12},{4,8},{8,4},{12,0},{16,28},{20,24},{24,20},{28,16},{1,13},{... | collective-permute-start | bytes 1572872 | tf_op jit(solution)/shard_map/ppermute | solution.py:409

commit v3 on v2

--- a/solution.py
+++ b/solution.py
@@ -43,38 +43,54 @@
     outs, (lines, mixed, sems) = refs[-len(plan) - 3 : -3], refs[-3:]
     tiles = side_size // 2
     chunks = sorted({chunk for targets in plan for _, chunk, _, _ in targets})
+    part_len = lines.shape[2] // PACK_PARTS
     loads = {}
     for chunk in chunks:
         for tile in range(tiles):
             columns = pl.ds((chunk * tiles + tile) * LANES, LANES)
-            slot = len(loads)
-            loads[chunk, tile] = pltpu.make_async_copy(
-                in_hbm.at[:, :, columns], lines.at[slot], sems.at[slot]
-            )
-            loads[chunk, tile].start()
+            for part in range(PACK_PARTS):
+                rows = pl.ds(part * part_len, part_len)
+                slot = len(loads)
+                loads[chunk, tile, part] = pltpu.make_async_copy(
+                    in_hbm.at[:, rows, columns],
+                    lines.at[slot // PACK_PARTS, :, rows],
+                    sems.at[slot],
+                )
+                loads[chunk, tile, part].start()
     stores = []
+
+    def send(index, chunk, owners, rows):
+        for out, targets in zip(outs, plan):
+            for spot, own_chunk, owner, relative in targets:
+                if own_chunk != chunk or relative != (owners is None):
+                    continue
+                if relative:
+                    owner = lax.bitwise_xor(meta_ref[0], owner)
+                elif owner not in owners:
+                    continue
+                source = mixed.at[index, owner, rows]
+                sem = sems.at[len(loads) + len(stores)]
+                stores.append(pltpu.make_async_copy(source, out.at[spot].at[rows], sem))
+                stores[-1].start()
+
     for index, chunk in enumerate(chunks):
         for tile in range(tiles):
-            loads[chunk, tile].wait()
-            slot = index * tiles + tile
-            first, second = lines[slot, 0], lines[slot, 1]
-            low = low_lanes(first.shape)
-            moved = swap_halves(jnp.where(low, second, first))
-            mixed[index, 2 * tile] = jnp.where(low, first, moved)
-            mixed[index, 2 * tile + 1] = jnp.where(low, moved, second)
-        for out, targets in zip(outs, plan):
-            for spot, own_chunk, owner, relative in targets:
-                if own_chunk == chunk:
-                    if relative:
-                        owner = lax.bitwise_xor(meta_ref[0], owner)
-                    stores.append(
-                        pltpu.make_async_copy(
-                            mixed.at[index, owner], out.at[spot], sems.at[len(loads) + len(stores)]
-                        )
-                    )
-                    stores[-1].start()
+            for part in range(PACK_PARTS):
+                rows = pl.ds(part * part_len, part_len)
+                loads[chunk, tile, part].wait()
+                slot = index * tiles + tile
+                first, second = lines[slot, 0, rows], lines[slot, 1, rows]
+                low = low_lanes(first.shape)
+                moved = swap_halves(jnp.where(low, second, first))
+                mixed[index, 2 * tile, rows] = jnp.where(low, first, moved)
+                mixed[index, 2 * tile + 1, rows] = jnp.where(low, moved, second)
+                send(index, chunk, (2 * tile, 2 * tile + 1), rows)
+        send(index, chunk, None, pl.ds(0, lines.shape[2]))
     for store in stores:
         store.wait()
+
+
+PACK_PARTS = 2
 
 
 def pack_lines(meta, packed, side_size, plan, shapes):
@@ -94,7 +110,7 @@
         scratch_shapes=[
             pltpu.VMEM((chunks * tiles, 2, block_len, LANES), jnp.float32),
             pltpu.VMEM((chunks, side_size, block_len, LANES), jnp.float32),
-            pltpu.SemaphoreType.DMA((chunks * tiles + copies,)),
+            pltpu.SemaphoreType.DMA((PACK_PARTS * (chunks * tiles + copies),)),
         ],
         cost_estimate=pl.CostEstimate(
             flops=0,
@@ -136,7 +152,12 @@
 
 def contract(matrices, start, depth, blocks, split_high, split_low, store):
     span = depth // len(blocks)
-    high, low = (ref[:, pl.ds(start, depth)] for ref in matrices)
+    both = None
+    if len(matrices) == 1:
+        both = matrices[0][:, pl.ds(2 * start, 2 * depth)]
+        high = matrices[0][:, pl.ds(2 * start, depth)]
+    else:
+        high, low = (ref[:, pl.ds(start, depth)] for ref in matrices)
     dot = functools.partial(jnp.dot, preferred_element_type=jnp.float32)
     for pair in range(RADIX // 2):
         columns = slice(2 * pair * LANES, 2 * (pair + 1) * LANES)
@@ -147,12 +168,17 @@
                 value = ref[index, pl.ds(digit, span, stride=RADIX), :]
                 top = value.astype(jnp.bfloat16)
                 split_high[rows, own] = top
+                if both is not None:
+                    split_high[pl.ds(depth + place * span, span), own] = top
                 split_low[rows, own] = (value - top.astype(jnp.float32)).astype(jnp.bfloat16)
-        total = dot(high, split_high[:, columns]) + dot(high, split_low[:, columns])
-        store(columns, total + dot(low, split_high[:, columns]))
-
-
-def begin_kernel(meta_ref, high_ref, low_ref, near_ref, out_ref, split_high, split_low):
+        if both is None:
+            total = dot(high, split_high[:, columns]) + dot(high, split_low[:, columns])
+            store(columns, total + dot(low, split_high[:, columns]))
+        else:
+            store(columns, dot(both, split_high[:, columns]) + dot(high, split_low[:, columns]))
+
+
+def begin_kernel(meta_ref, both_ref, near_ref, out_ref, split_high, split_low):
     side_size = near_ref.shape[0]
     depth = SUB // 2
     start = pl.multiple_of(meta_ref[1] * depth, depth)
@@ -161,23 +187,26 @@
     def store(columns, value):
         out_ref[:, columns] = value
 
-    contract((high_ref, low_ref), start, depth, blocks, split_high, split_low, store)
-
-
-def begin(meta, tables, near):
+    contract((both_ref,), start, depth, blocks, split_high, split_low, store)
+
+
+def begin(meta, both, near):
     vmem = pl.BlockSpec(memory_space=pltpu.VMEM)
     return pl.pallas_call(
         begin_kernel,
-        in_specs=[pl.BlockSpec(memory_space=pltpu.SMEM)] + [vmem] * 3,
+        in_specs=[pl.BlockSpec(memory_space=pltpu.SMEM)] + [vmem] * 2,
         out_specs=vmem,
         out_shape=jax.ShapeDtypeStruct((2 * SUB, RADIX * LANES), jnp.float32),
-        scratch_shapes=[pltpu.VMEM((SUB // 2, RADIX * LANES), jnp.bfloat16)] * 2,
+        scratch_shapes=[
+            pltpu.VMEM((SUB, RADIX * LANES), jnp.bfloat16),
+            pltpu.VMEM((SUB // 2, RADIX * LANES), jnp.bfloat16),
+        ],
         compiler_params=pltpu.CompilerParams(vmem_limit_bytes=16 * MIB),
         cost_estimate=pl.CostEstimate(
             flops=6 * SUB * SUB * RADIX * LANES, transcendentals=0, bytes_accessed=5 * MIB
         ),
         name="begin",
-    )(meta, *tables[:2], near)
+    )(meta, both, near)
 
 
 def transform_kernel(
@@ -207,7 +236,8 @@
     def store(columns, value):
         product[:, columns] = inputs[0][:, columns] + value if begun else value
 
-    contract((high_ref, low_ref), start, depth, blocks, split_high, split_low, store)
+    matrices = (high_ref,) if begun else (high_ref, low_ref)
+    contract(matrices, start, depth, blocks, split_high, split_low, store)
 
     own_place = meta_ref[0]
     side_float = meta_ref[1].astype(jnp.float32)
@@ -260,7 +290,7 @@
     parts = 2
     for part in range(parts):
         steps = SUB // 8 // parts
-        lax.fori_loop(part * steps, (part + 1) * steps, rows_body, 0, unroll=4)
+        lax.fori_loop(part * steps, (part + 1) * steps, rows_body, 0, unroll=8)
         rows = pl.ds(part * SUB // parts, SUB // parts)
         for step in range(side_size):
             owner = lax.bitwise_xor(own_place, step)
@@ -289,7 +319,7 @@
         out_specs=[hbm] * side_size,
         out_shape=[block] * side_size,
         scratch_shapes=[
-            pltpu.VMEM((depth, RADIX * LANES), jnp.bfloat16),
+            pltpu.VMEM((SUB, RADIX * LANES), jnp.bfloat16),
             pltpu.VMEM((depth, RADIX * LANES), jnp.bfloat16),
             pltpu.VMEM((2 * SUB, RADIX * LANES), jnp.float32),
             pltpu.VMEM((HALF_RADIX, 2, SUB, LANES), jnp.float32),
@@ -376,6 +406,10 @@
     high, low, twiddle = dft_tables()
     twiddle = jnp.broadcast_to(jnp.asarray(twiddle.T)[:, :, None], (2 * RADIX, SUB, LANES))
     tables = [jnp.asarray(high), jnp.asarray(low), twiddle]
+    halves = [
+        table[:, part : part + SUB // 2] for part in (0, SUB // 2) for table in (high, low)
+    ]
+    both = jnp.asarray(np.concatenate(halves, axis=1))
     wave_y = wave_y.reshape(pencils // LANES, LANES)
     wave_z = wave_z.reshape(pencils // LANES, LANES)
 
@@ -399,10 +433,11 @@
         got, others = lax.optimization_barrier((got, others))
         lines[0] = [got]
         held = jnp.concatenate([sends[0], others])
-        lines.append([begin(meta, tables, held), early, swap(others, side_size)])
+        lines.append([begin(meta, both, held), early, swap(others, side_size)])
     result = None
     for chunk in range(chunks):
-        blocks = transform(meta, wave_y, wave_z, tables, lines[chunk], chunk, side_size)
+        own_tables = tables if chunk == 0 else [both, *tables[1:]]
+        blocks = transform(meta, wave_y, wave_z, own_tables, lines[chunk], chunk, side_size)
         blocks = [
             block
             if step == 0

time: 139 us -> 139 us (level)
  Pallas kernels: 25.8 us -> 24.1 us
  transfers between devices with their start and end apart: 12 -> 12, of which waited for: 7 -> 7; matrix products, arithmetic and copies ran while one was open for 1% -> 1% of each run, Pallas kernels for 15% -> 14%
where the time goes in v3:
time: 139 us; the launch traced here: 138 us
  waiting for transfers between devices  91.3 us (66%)
  Pallas kernels  24.1 us (17%)
  starting transfers between devices  20.9 us (15%)
    ppermute x5, waiting for transfers between devices, swap(): return lax.ppermute(value, 'gx', [(i, i ^ step) for i in range(cycle_size)])  71.1 us
    ppermute x6, waiting for transfers between devices, shards(): lax.ppermute(block, 'gx', [(i, i ^ step) for i in range(cycle_size)])  18.3 us
    pallas_call x2, Pallas kernels, transform(): pl.pallas_call(functools.partial(transform_kernel, chunk=chunk, side_size...  9.57 us
    ppermute x5, starting transfers between devices, swap(): return lax.ppermute(value, 'gx', [(i, i ^ step) for i in range(cycle_size)])  7.42 us
    all_to_all x1, starting transfers between devices, shards(): lax.all_to_all(send.reshape(cycle_size, block_len, LANES), 'gx', split_ax...  7.26 us
    pallas_call x4, Pallas kernels, place(): pl.pallas_call(functools.partial(place_kernel, chunk=chunk, step=step, si...  6.8 us
    ppermute x6, starting transfers between devices, shards(): lax.ppermute(block, 'gx', [(i, i ^ step) for i in range(cycle_size)])  6.22 us
    pallas_call x2, Pallas kernels, pack_lines(): pl.pallas_call(functools.partial(pack_kernel, side_size=side_size, plan=p...  5.8 us
  transfers between devices with their start and end apart: 12, of which 7 were waited for; matrix products, arithmetic and copies ran while one was open for 1% of the time, Pallas kernels for 14%

profile of v3, /device:TPU:0, one launch (start us, length us, event | category | flops | bytes accessed | tf_op | source)
XLA Modules:
  0.0 138.5 jit_solution(12691432065629734287)
XLA Ops:
  0.0 2.5 %pack_lines.2 = f32[2,4,512,128]{3,2,1,0:T(8,128)} custom-call(f32[2,512,512]{2,1,0:T(8,128)} %refs_1_), custom_call_target="tpu_custom_call" | custom-call | bytes 3145728 | tf_op jit(solution)/shard_map/pack_lines/pallas_call | solution.py:103
  2.6 7.3 %all-to-all-start = ((f32[8,512,128]{2,1,0:T(8,128)}), f32[8,512,128]{2,1,0:T(8,128)S(1)}, u32[]{:S(2)}, u32[]{:S(2)}) async-start(f32[8,512,128]{2,1,0:T(8,128)} %bitcast.9), calls=%async_computation | async-start | bytes 4194304 | tf_op jit(solution)/shard_map/all_to_all | solution.py:422
  10.5 3.3 %pack_lines.3 = (f32[1,512,128]{2,1,0:T(8,128)}, f32[1,512,128]{2,1,0:T(8,128)}, f32[1,512,128]{2,1,0:T(8,128)}, f32[1,512,128]{2,1,0:T(8,128)}) custom-call(s32[2]{0:T(128)} %pad_add_fusion.refs_0_.meta_ref, f32[2,512,512]{2,1,0:T(8,128)} %refs_1_), custom_call_target="tpu_custom_call" | custom-call | bytes 2097152 | tf_op jit(solution)/shard_map/pack_lines/pallas_call | solution.py:103
  13.8 2.1 %collective-permute-start = (f32[1,512,128]{2,1,0:T(8,128)}, f32[1,512,128]{2,1,0:T(8,128)S(1)}, u32[]{:S(2)}, u32[]{:S(2)}) collective-permute-start(f32[1,512,128]{2,1,0:T(8,128)} %get-tuple-element.22), channel_id=1, source_target_pairs={{0,4},{4,0},{8,12},{12,8},{16,20},{20,16},{24,28},{28,24},{1,5},{5... | collective-permute-start | bytes 786440 | tf_op jit(solution)/shard_map/ppermute | solution.py:417
  15.8 1.5 %collective-permute-start.1 = (f32[1,512,128]{2,1,0:T(8,128)}, f32[1,512,128]{2,1,0:T(8,128)S(1)}, u32[]{:S(2)}, u32[]{:S(2)}) collective-permute-start(f32[1,512,128]{2,1,0:T(8,128)} %get-tuple-element.23), channel_id=1, source_target_pairs={{0,8},{4,12},{8,0},{12,4},{16,24},{20,28},{24,16},{28,20},{1,9},{5... | collective-permute-start | bytes 786440 | tf_op jit(solution)/shard_map/ppermute | solution.py:417
  17.4 16.4 %collective-permute-done = f32[1,512,128]{2,1,0:T(8,128)S(1)} collective-permute-done((f32[1,512,128]{2,1,0:T(8,128)}, f32[1,512,128]{2,1,0:T(8,128)S(1)}, u32[]{:S(2)}, u32[]{:S(2)}) %collective-permute-start) | collective-permute-done | bytes 262176 | tf_op jit(solution)/shard_map/ppermute | solution.py:417
  33.8 17.9 %collective-permute-done.1 = f32[1,512,128]{2,1,0:T(8,128)S(1)} collective-permute-done((f32[1,512,128]{2,1,0:T(8,128)}, f32[1,512,128]{2,1,0:T(8,128)S(1)}, u32[]{:S(2)}, u32[]{:S(2)}) %collective-permute-start.1) | collective-permute-done | bytes 262176 | tf_op jit(solution)/shard_map/ppermute | solution.py:417
  51.7 4.5 %collective-permute-done.2 = f32[1,512,128]{2,1,0:T(8,128)S(1)} collective-permute-done((f32[1,512,128]{2,1,0:T(8,128)}, f32[1,512,128]{2,1,0:T(8,128)S(1)}, u32[]{:S(2)}, u32[]{:S(2)}) %collective-permute-start.2) | collective-permute-done | bytes 262176 | tf_op jit(solution)/shard_map/ppermute | solution.py:417
  56.2 1.9 %all-to-all-done.rest_0_ = f32[8,512,128]{2,1,0:T(8,128)S(1)} async-done(((f32[8,512,128]{2,1,0:T(8,128)}), f32[8,512,128]{2,1,0:T(8,128)S(1)}, u32[]{:S(2)}, u32[]{:S(2)}) %all-to-all-start) | async-done | bytes 2097184 | tf_op jit(solution)/shard_map/all_to_all | solution.py:422
  58.1 2.6 %collective-permute-start.4 = (f32[3,512,128]{2,1,0:T(8,128)S(1)}, f32[3,512,128]{2,1,0:T(8,128)S(1)}, u32[]{:S(2)}, u32[]{:S(2)}) collective-permute-start(f32[3,512,128]{2,1,0:T(8,128)S(1)} %pad_maximum_fusion.1), channel_id=1, source_target_pairs={{0,16},{4,20},{8,24},{12,28},{16,0},{20,4},{24,8},{28,12},{1,17},{... | collective-permute-start | bytes 2359304 | tf_op jit(solution)/shard_map/ppermute | solution.py:417
  61.9 5.1 %transform.3 = (f32[2,2,256,128]{3,2,1,0:T(8,128)S(1)}, f32[2,2,256,128]{3,2,1,0:T(8,128)S(1)}, f32[2,2,256,128]{3,2,1,0:T(8,128)S(1)}, f32[2,2,256,128]{3,2,1,0:T(8,128)S(1)}) custom-call(s32[2]{0:T(128)S(1)} %copy-done.3, s32[4,128]{1,0:T(4,128)S(1)} %bitcast.5, s32[4,128]{1,0:T(4,128)S(1)} %bitcast.7, bf16[512,256]{1,0:T(8,128)(2,1)S(1)} %copy-done.2, ...), custom_call_target="tpu_custom_call" | custom-call | flops 1610612736 | bytes 5242880 | tf_op jit(solution)/shard_map/transform/pallas_call | solution.py:316
  67.6 1.2 collective-permute-start.3
  69.4 1.4 %collective-permute-start.9 = (f32[2,2,256,128]{3,2,1,0:T(8,128)S(1)}, f32[2,2,256,128]{3,2,1,0:T(8,128)S(1)}, u32[]{:S(2)}, u32[]{:S(2)}) collective-permute-start(f32[2,2,256,128]{3,2,1,0:T(8,128)S(1)} %get-tuple-element.32), channel_id=1, source_target_pairs={{0,12},{4,8},{8,4},{12,0},{16,28},{20,24},{24,20},{28,16},{1,13},{... | collective-permute-start | bytes 1572872 | tf_op jit(solution)/shard_map/ppermute | solution.py:444
  71.0 2.0 %begin.1.rest_0_ = f32[512,2048]{1,0:T(8,128)S(1)} custom-call(s32[2]{0:T(128)S(1)} %copy-done.3, bf16[512,512]{1,0:T(8,128)(2,1)S(1)} %copy-done, f32[4,512,128]{2,1,0:T(8,128)S(1)} %pad_maximum_fusion.near_ref), custom_call_target="tpu_custom_call" | custom-call | flops 805306368 | bytes 5242880 | tf_op jit(solution)/shard_map/begin/pallas_call | solution.py:195
  72.9 32.3 %collective-permute-done.3.rest_1_ = f32[1,512,128]{2,1,0:T(8,128)S(1)} collective-permute-done((f32[1,512,128]{2,1,0:T(8,128)S(1)}, f32[1,512,128]{2,1,0:T(8,128)S(1)}, u32[]{:S(2)}, u32[]{:S(2)}) %collective-permute-start.3) | collective-permute-done | bytes 262176 | tf_op jit(solution)/shard_map/ppermute | solution.py:417
  105.3 4.4 %transform.2 = (f32[2,2,256,128]{3,2,1,0:T(8,128)S(1)}, f32[2,2,256,128]{3,2,1,0:T(8,128)S(1)}, f32[2,2,256,128]{3,2,1,0:T(8,128)S(1)}, f32[2,2,256,128]{3,2,1,0:T(8,128)S(1)}) custom-call(s32[2]{0:T(128)S(1)} %copy-done.3, s32[4,128]{1,0:T(4,128)S(1)} %bitcast.6, s32[4,128]{1,0:T(4,128)S(1)} %bitcast.8, bf16[512,512]{1,0:T(8,128)(2,1)S(1)} %copy-done, ...), custom_call_target="tpu_custom_call" | custom-call | flops 1610612736 | bytes 5242880 | tf_op jit(solution)/shard_map/transform/pallas_call | solution.py:316
  109.7 1.8 %collective-permute-start.7 = (f32[2,2,256,128]{3,2,1,0:T(8,128)S(1)}, f32[2,2,256,128]{3,2,1,0:T(8,128)S(1)}, u32[]{:S(2)}, u32[]{:S(2)}) collective-permute-start(f32[2,2,256,128]{3,2,1,0:T(8,128)S(1)} %get-tuple-element.29), channel_id=1, source_target_pairs={{0,4},{4,0},{8,12},{12,8},{16,20},{20,16},{24,28},{28,24},{1,5},{5... | collective-permute-start | bytes 1572872 | tf_op jit(solution)/shard_map/ppermute | solution.py:444
  111.6 1.7 %collective-permute-start.6 = (f32[2,2,256,128]{3,2,1,0:T(8,128)S(1)}, f32[2,2,256,128]{3,2,1,0:T(8,128)S(1)}, u32[]{:S(2)}, u32[]{:S(2)}) collective-permute-start(f32[2,2,256,128]{3,2,1,0:T(8,128)S(1)} %get-tuple-element.27), channel_id=1, source_target_pairs={{0,12},{4,8},{8,4},{12,0},{16,28},{20,24},{24,20},{28,16},{1,13},{... | collective-permute-start | bytes 1572872 | tf_op jit(solution)/shard_map/ppermute | solution.py:444
  113.3 1.7 %place.4.rest_0_ = f32[2,2,512,512]{3,2,1,0:T(8,128)} custom-call(s32[2]{0:T(128)S(1)} %copy-done.3, f32[2,2,256,128]{3,2,1,0:T(8,128)S(1)} %get-tuple-element.33.even_ref, f32[2,2,256,128]{3,2,1,0:T(8,128)S(1)} %collective-permute-done.10.odd_ref), custom_call_target="tpu_custom_call" | custom-call | bytes 2097152 | tf_op jit(solution)/shard_map/place/pallas_call | solution.py:379
  115.0 1.7 %place.5.rest_0_ = f32[2,2,512,512]{3,2,1,0:T(8,128)} custom-call(s32[2]{0:T(128)S(1)} %copy-done.3, f32[2,2,256,128]{3,2,1,0:T(8,128)S(1)} %collective-permute-done.8.even_ref, f32[2,2,256,128]{3,2,1,0:T(8,128)S(1)} %collective-permute-done.9.odd_ref, f32[2,2,512,512]{3,2,1,0:T(8,128)} %place.4.rest_0_), custom_call_target="tpu_custom_call", output_to_operand_aliasing={{}: (3, {})} | custom-call | bytes 2097152 | tf_op jit(solution)/shard_map/place/pallas_call | solution.py:379
  116.7 9.4 %collective-permute-done.7.odd_ref = f32[2,2,256,128]{3,2,1,0:T(8,128)S(1)} collective-permute-done((f32[2,2,256,128]{3,2,1,0:T(8,128)S(1)}, f32[2,2,256,128]{3,2,1,0:T(8,128)S(1)}, u32[]{:S(2)}, u32[]{:S(2)}) %collective-permute-start.7) | collective-permute-done | bytes 524320 | tf_op jit(solution)/shard_map/ppermute | solution.py:444
  126.2 1.7 %place.6.rest_0_ = f32[2,2,512,512]{3,2,1,0:T(8,128)} custom-call(s32[2]{0:T(128)S(1)} %copy-done.3, f32[2,2,256,128]{3,2,1,0:T(8,128)S(1)} %get-tuple-element.28.even_ref, f32[2,2,256,128]{3,2,1,0:T(8,128)S(1)} %collective-permute-done.7.odd_ref, f32[2,2,512,512]{3,2,1,0:T(8,128)} %place.5.rest_0_), custom_call_target="tpu_custom_call", output_to_operand_aliasing={{}: (3, {})} | custom-call | bytes 2097152 | tf_op jit(solution)/shard_map/place/pallas_call | solution.py:379
  127.9 8.9 %collective-permute-done.6.odd_ref = f32[2,2,256,128]{3,2,1,0:T(8,128)S(1)} collective-permute-done((f32[2,2,256,128]{3,2,1,0:T(8,128)S(1)}, f32[2,2,256,128]{3,2,1,0:T(8,128)S(1)}, u32[]{:S(2)}, u32[]{:S(2)}) %collective-permute-start.6) | collective-permute-done | bytes 524320 | tf_op jit(solution)/shard_map/ppermute | solution.py:444
  136.8 1.7 %place.7 = f32[2,2,512,512]{3,2,1,0:T(8,128)} custom-call(s32[2]{0:T(128)S(1)} %copy-done.3, f32[2,2,256,128]{3,2,1,0:T(8,128)S(1)} %collective-permute-done.5.even_ref, f32[2,2,256,128]{3,2,1,0:T(8,128)S(1)} %collective-permute-done.6.odd_ref, f32[2,2,512,512]{3,2,1,0:T(8,128)} %place.6.rest_0_), custom_call_target="tpu_custom_call", output_to_operand_aliasing={{}: (3, {})} | custom-call | bytes 2097152 | tf_op jit(solution)/shard_map/place/pallas_call | solution.py:379
  (29 shorter events, 3.2 us)
Async XLA Ops:
  2.5 58.1 %copy-start.7 = (f32[32,256]{1,0:T(8,128)S(1)}, f32[32,256]{1,0:T(8,128)}, u32[]{:S(2)}) copy-start(f32[32,256]{1,0:T(8,128)} %constant.30.clone) | copy-start | bytes 98308
  2.6 55.5 %all-to-all-start = ((f32[8,512,128]{2,1,0:T(8,128)}), f32[8,512,128]{2,1,0:T(8,128)S(1)}, u32[]{:S(2)}, u32[]{:S(2)}) async-start(f32[8,512,128]{2,1,0:T(8,128)} %bitcast.9), calls=%async_computation | async-start | bytes 4194304 | tf_op jit(solution)/shard_map/all_to_all | solution.py:422
  9.8 52.0 %copy-start.1 = (bf16[512,256]{1,0:T(8,128)(2,1)S(1)}, bf16[512,256]{1,0:T(8,128)(2,1)}, u32[]{:S(2)}) copy-start(bf16[512,256]{1,0:T(8,128)(2,1)} %constant.32.clone.low_ref) | copy-start | bytes 786436
  9.8 52.0 %copy-start.2 = (bf16[512,256]{1,0:T(8,128)(2,1)S(1)}, bf16[512,256]{1,0:T(8,128)(2,1)}, u32[]{:S(2)}) copy-start(bf16[512,256]{1,0:T(8,128)(2,1)} %constant.31.clone.high_ref) | copy-start | bytes 786436
  9.8 52.0 %copy-start.4 = (s32[512]{0:T(512)S(1)}, s32[512]{0:T(512)}, u32[]{:S(2)}) copy-start(s32[512]{0:T(512)} %param.8) | copy-start | bytes 6148
  9.8 52.0 %copy-start.5 = (s32[512]{0:T(512)S(1)}, s32[512]{0:T(512)}, u32[]{:S(2)}) copy-start(s32[512]{0:T(512)} %param.9) | copy-start | bytes 6148
  10.5 51.3 %copy-start.3 = (s32[2]{0:T(128)S(1)}, s32[2]{0:T(128)}, u32[]{:S(2)}) copy-start(s32[2]{0:T(128)} %pad_add_fusion.refs_0_.meta_ref) | copy-start | bytes 28
  13.8 20.0 %collective-permute-start = (f32[1,512,128]{2,1,0:T(8,128)}, f32[1,512,128]{2,1,0:T(8,128)S(1)}, u32[]{:S(2)}, u32[]{:S(2)}) collective-permute-start(f32[1,512,128]{2,1,0:T(8,128)} %get-tuple-element.22), channel_id=1, source_target_pairs={{0,4},{4,0},{8,12},{12,8},{16,20},{20,16},{24,28},{28,24},{1,5},{5... | collective-permute-start | bytes 786440 | tf_op jit(solution)/shard_map/ppermute | solution.py:417
  15.8 35.8 %collective-permute-start.1 = (f32[1,512,128]{2,1,0:T(8,128)}, f32[1,512,128]{2,1,0:T(8,128)S(1)}, u32[]{:S(2)}, u32[]{:S(2)}) collective-permute-start(f32[1,512,128]{2,1,0:T(8,128)} %get-tuple-element.23), channel_id=1, source_target_pairs={{0,8},{4,12},{8,0},{12,4},{16,24},{20,28},{24,16},{28,20},{1,9},{5... | collective-permute-start | bytes 786440 | tf_op jit(solution)/shard_map/ppermute | solution.py:417
  17.3 38.8 %collective-permute-start.2 = (f32[1,512,128]{2,1,0:T(8,128)}, f32[1,512,128]{2,1,0:T(8,128)S(1)}, u32[]{:S(2)}, u32[]{:S(2)}) collective-permute-start(f32[1,512,128]{2,1,0:T(8,128)} %get-tuple-element.24), channel_id=1, source_target_pairs={{0,12},{4,8},{8,4},{12,0},{16,28},{20,24},{24,20},{28,16},{1,13},{... | collective-permute-start | bytes 786440 | tf_op jit(solution)/shard_map/ppermute | solution.py:417
  58.1 47.2 %collective-permute-start.4 = (f32[3,512,128]{2,1,0:T(8,128)S(1)}, f32[3,512,128]{2,1,0:T(8,128)S(1)}, u32[]{:S(2)}, u32[]{:S(2)}) collective-permute-start(f32[3,512,128]{2,1,0:T(8,128)S(1)} %pad_maximum_fusion.1), channel_id=1, source_target_pairs={{0,16},{4,20},{8,24},{12,28},{16,0},{20,4},{24,8},{28,12},{1,17},{... | collective-permute-start | bytes 2359304 | tf_op jit(solution)/shard_map/ppermute | solution.py:417
  61.8 5.8 %copy-start.6 = (f32[1,512,128]{2,1,0:T(8,128)S(1)}, f32[1,512,128]{2,1,0:T(8,128)}, u32[]{:S(2)}) copy-start(f32[1,512,128]{2,1,0:T(8,128)} %get-tuple-element.21) | copy-start | bytes 786436
  61.8 9.1 %copy-start = (bf16[512,512]{1,0:T(8,128)(2,1)S(1)}, bf16[512,512]{1,0:T(8,128)(2,1)}, u32[]{:S(2)}) copy-start(bf16[512,512]{1,0:T(8,128)(2,1)} %constant.33.clone.both_ref.high_ref) | copy-start | bytes 1572868
  67.0 44.6 %collective-permute-start.10 = (f32[2,2,256,128]{3,2,1,0:T(8,128)S(1)}, f32[2,2,256,128]{3,2,1,0:T(8,128)S(1)}, u32[]{:S(2)}, u32[]{:S(2)}) collective-permute-start(f32[2,2,256,128]{3,2,1,0:T(8,128)S(1)} %get-tuple-element.34), channel_id=1, source_target_pairs={{0,4},{4,0},{8,12},{12,8},{16,20},{20,16},{24,28},{28,24},{1,5},{5... | collective-permute-start | bytes 1572872 | tf_op jit(solution)/shard_map/ppermute | solution.py:444
  67.6 37.6 %collective-permute-start.3 = (f32[1,512,128]{2,1,0:T(8,128)S(1)}, f32[1,512,128]{2,1,0:T(8,128)S(1)}, u32[]{:S(2)}, u32[]{:S(2)}) collective-permute-start(f32[1,512,128]{2,1,0:T(8,128)S(1)} %copy-done.6), channel_id=1, source_target_pairs={{0,16},{4,20},{8,24},{12,28},{16,0},{20,4},{24,8},{28,12},{1,17},{... | collective-permute-start | bytes 786440 | tf_op jit(solution)/shard_map/ppermute | solution.py:417
  68.9 46.1 %collective-permute-start.8 = (f32[2,2,256,128]{3,2,1,0:T(8,128)S(1)}, f32[2,2,256,128]{3,2,1,0:T(8,128)S(1)}, u32[]{:S(2)}, u32[]{:S(2)}) collective-permute-start(f32[2,2,256,128]{3,2,1,0:T(8,128)S(1)} %get-tuple-element.31), channel_id=1, source_target_pairs={{0,8},{4,12},{8,0},{12,4},{16,24},{20,28},{24,16},{28,20},{1,9},{5... | collective-permute-start | bytes 1572872 | tf_op jit(solution)/shard_map/ppermute | solution.py:444
  69.4 45.6 %collective-permute-start.9 = (f32[2,2,256,128]{3,2,1,0:T(8,128)S(1)}, f32[2,2,256,128]{3,2,1,0:T(8,128)S(1)}, u32[]{:S(2)}, u32[]{:S(2)}) collective-permute-start(f32[2,2,256,128]{3,2,1,0:T(8,128)S(1)} %get-tuple-element.32), channel_id=1, source_target_pairs={{0,12},{4,8},{8,4},{12,0},{16,28},{20,24},{24,20},{28,16},{1,13},{... | collective-permute-start | bytes 1572872 | tf_op jit(solution)/shard_map/ppermute | solution.py:444
  109.7 16.4 %collective-permute-start.7 = (f32[2,2,256,128]{3,2,1,0:T(8,128)S(1)}, f32[2,2,256,128]{3,2,1,0:T(8,128)S(1)}, u32[]{:S(2)}, u32[]{:S(2)}) collective-permute-start(f32[2,2,256,128]{3,2,1,0:T(8,128)S(1)} %get-tuple-element.29), channel_id=1, source_target_pairs={{0,4},{4,0},{8,12},{12,8},{16,20},{20,16},{24,28},{28,24},{1,5},{5... | collective-permute-start | bytes 1572872 | tf_op jit(solution)/shard_map/ppermute | solution.py:444
  111.6 16.3 %collective-permute-start.5 = (f32[2,2,256,128]{3,2,1,0:T(8,128)S(1)}, f32[2,2,256,128]{3,2,1,0:T(8,128)S(1)}, u32[]{:S(2)}, u32[]{:S(2)}) collective-permute-start(f32[2,2,256,128]{3,2,1,0:T(8,128)S(1)} %get-tuple-element.26), channel_id=1, source_target_pairs={{0,8},{4,12},{8,0},{12,4},{16,24},{20,28},{24,16},{28,20},{1,9},{5... | collective-permute-start | bytes 1572872 | tf_op jit(solution)/shard_map/ppermute | solution.py:444
  111.6 25.2 %collective-permute-start.6 = (f32[2,2,256,128]{3,2,1,0:T(8,128)S(1)}, f32[2,2,256,128]{3,2,1,0:T(8,128)S(1)}, u32[]{:S(2)}, u32[]{:S(2)}) collective-permute-start(f32[2,2,256,128]{3,2,1,0:T(8,128)S(1)} %get-tuple-element.27), channel_id=1, source_target_pairs={{0,12},{4,8},{8,4},{12,0},{16,28},{20,24},{24,20},{28,16},{1,13},{... | collective-permute-start | bytes 1572872 | tf_op jit(solution)/shard_map/ppermute | solution.py:444
